TPU v7x, 32 devices: a whole 2x2x4 slice. The times are simulated.
32 devices in a mesh: grp: 2 (over y), seq: 4 (over z), zero: 4 (over x, core).
Axes of the slice: x: 2, y: 2, z: 4, core: 2. Of those that a mesh axis runs over, the one named last changes fastest.
Arguments:
- hidden: bfloat16 [8, 512, 1280], P(('grp', 'zero'), 'seq'), parts along dimension 0, may hold values from -6 to 6
- grad_out: bfloat16 [8, 512, 1280], P(('grp', 'zero'), 'seq'), parts along dimension 0, may hold values from -6 to 6
- w_proj: bfloat16 [1280, 148], P('zero'), may hold values from -0.15625 to 0.15625
- conv_w: bfloat16 [4, 1408], P(None, 'zero'), may hold values from -3 to 3
- a_log: float32 [20], replicated, may hold values from -8 to 1, as said below
- dt_bias: float32 [20], replicated, may hold values from -4.5 to -3
Outputs:
- output: bfloat16 [8, 512, 1280], P(('grp', 'zero'), 'seq'), parts along dimension 0
- grad_hidden: bfloat16 [8, 512, 1280], P(('grp', 'zero'), 'seq'), parts along dimension 0
- grad_proj: float32 [2560, 148], P(('grp', 'zero')), parts along dimension 0
- grad_conv: float32 [8, 1408], P('grp', 'zero'), parts along dimension 0
- grad_heads: float32 [4, 20], P('grp'), parts along dimension 0
There are 2 independent parts, one for each index of `grp`. A program takes and returns all parts, laid end to end along the dimension named above; an argument that names none is the same for every part. Nothing has to cross between parts.
Inputs may be any that keep to these rules, and one draw needn't show every extreme that they name: `a_log`: the logarithms of the heads' decay rates.
All inputs are finite; a program needn't handle non-finite values.
Results may differ from a plain program's by a relative error of at most 0.017.
Values may be sent and summed in bfloat16 or wider, within the bound.
A program may use at most 192 MiB of HBM per device.

v0:
```python
import jax
import jax.numpy as jnp
from jax import lax
from jax.sharding import PartitionSpec as P

WIDTH = 1280
STATE = 64
HEAD_DIM = 64
SPAN = 128
KERNEL = 4


def prefix(x, axis, join, neutral, backward):
    count = lax.axis_size(axis)
    place = lax.axis_index(axis)
    ahead = count - 1 - place if backward else place
    gathered = jax.tree.map(
        lambda a, kind: lax.all_gather(a.astype(kind), axis),
        x,
        jax.tree.map(lambda a: jnp.bfloat16 if a.dtype == jnp.float32 else a.dtype, x),
    )
    state = jax.tree.map(lambda a, e: jnp.zeros_like(a) + jnp.asarray(e, a.dtype), x, neutral)

    def one(hop, state):
        source = count - 1 - hop if backward else hop
        return join(
            state,
            jax.tree.map(
                lambda a, own: lax.dynamic_index_in_dim(a, source, 0, False).astype(own.dtype),
                gathered,
                x,
            ),
        )

    return lax.fori_loop(0, ahead, one, state)


def extended(x, sides, width):
    for axis, dim in sides:
        size, length = (lax.axis_size(axis), x.shape[dim])
        up = [(i, (i + 1) % size) for i in range(size - 1)]
        down = [(j, i) for i, j in up]
        last = lax.slice_in_dim(x, length - width, length, axis=dim)
        leading = lax.slice_in_dim(x, 0, width, axis=dim)
        before = lax.ppermute(last, axis, up)
        after = lax.ppermute(leading, axis, down)
        x = jnp.concatenate([before, x, after], axis=dim)
    return x


def combine_states(earlier, later):
    return (earlier[0] * later[0], later[0][..., None, None] * earlier[1] + later[1])


def pass_upward(pieces):
    identity = (jnp.ones_like(pieces[0]), jnp.zeros_like(pieces[1]))
    return prefix(pieces, "seq", combine_states, identity, False)[1]


def pass_downward(pieces):
    identity = (jnp.ones_like(pieces[0]), jnp.zeros_like(pieces[1]))
    return prefix(pieces, "seq", combine_states, identity, True)[1]


def conv_core(ahead_in, dt_raw, filters, a_log, dt_bias):
    length = dt_raw.shape[0]
    head_count = dt_raw.shape[1]
    blocks = length // SPAN
    mixed_sum = filters[0] * ahead_in[KERNEL - 1 : KERNEL - 1 + length]
    for step_back in range(1, KERNEL):
        mixed_sum = (
            mixed_sum
            + filters[step_back]
            * ahead_in[KERNEL - 1 - step_back : KERNEL - 1 - step_back + length]
        )
    active = jax.nn.silu(mixed_sum)
    values = active[:, :WIDTH].astype(jnp.bfloat16).reshape(blocks, SPAN, head_count, HEAD_DIM)
    b_mat = active[:, WIDTH : WIDTH + STATE].astype(jnp.bfloat16).reshape(blocks, SPAN, STATE)
    c_mat = active[:, WIDTH + STATE :].astype(jnp.bfloat16)
    c_blocks = c_mat.reshape(blocks, SPAN, STATE)
    steps_dt = jax.nn.softplus(dt_raw + dt_bias)
    log_decay = -jnp.exp(a_log) * steps_dt
    within = jnp.cumsum(log_decay.reshape(blocks, SPAN, head_count), axis=1).transpose(0, 2, 1)
    dt_blocks = steps_dt.reshape(blocks, SPAN, head_count).transpose(0, 2, 1)
    scores = jnp.einsum("kin,kjn->kij", c_blocks, b_mat, preferred_element_type=jnp.float32)
    causal = jnp.arange(SPAN)[:, None] >= jnp.arange(SPAN)[None, :]
    gap_log = within[:, :, :, None] - within[:, :, None, :]
    decays = jnp.exp(jnp.where(causal, gap_log, -jnp.inf))
    weights = (scores[:, None] * decays * dt_blocks[:, :, None, :]).astype(jnp.bfloat16)
    y_intra = jnp.einsum("khij,kjhp->kihp", weights, values, preferred_element_type=jnp.float32)
    to_end = jnp.exp(within[:, :, -1:] - within) * dt_blocks
    b_weighted = (to_end[..., None] * b_mat[:, None, :, :].astype(jnp.float32)).astype(jnp.bfloat16)
    states = jnp.einsum("khjn,kjhp->khnp", b_weighted, values, preferred_element_type=jnp.float32)
    totals = within[:, :, -1]

    def advance(carried, current):
        return (jnp.exp(current[0])[:, None, None] * carried + current[1], carried)

    last_state, entering = lax.scan(
        advance, jnp.zeros(states.shape[1:], jnp.float32), (totals, states)
    )
    y_inter = jnp.einsum(
        "kin,khnp->kihp", c_blocks.astype(jnp.float32), entering, precision=lax.Precision.HIGH
    )
    y_inter = y_inter * jnp.exp(within).transpose(0, 2, 1)[..., None]
    y_local = (y_intra + y_inter).reshape(length, WIDTH)
    offsets = jnp.cumsum(totals, axis=0) - totals
    reached = jnp.exp(within + offsets[:, :, None]).transpose(0, 2, 1).reshape(length, head_count)
    overall = jnp.exp(jnp.sum(totals, axis=0))
    return (y_local, overall, last_state, reached, c_mat)


def add_incoming(y_local, reached, c_mat, incoming):
    carried = jnp.einsum(
        "tn,hnp->thp", c_mat.astype(jnp.float32), incoming, precision=lax.Precision.HIGH
    )
    return y_local + (reached[:, :, None] * carried).reshape(y_local.shape)


def strand_pass(tokens, cotangent, w_full, filters, a_log, dt_bias):
    length = tokens.shape[1]
    margin = KERNEL - 1
    projected = jnp.einsum("std,dc->stc", tokens, w_full, preferred_element_type=jnp.float32)
    inner_act = jnp.concatenate([tokens, projected[..., : 2 * STATE].astype(jnp.bfloat16)], axis=2)
    dt_raw = projected[..., 2 * STATE :]
    padded = extended(inner_act, (("seq", 1),), margin)
    padded = padded.astype(jnp.float32)
    ahead_in = padded[:, : length + margin]
    behind = jnp.flip(padded[:, margin:], axis=1)
    core_batch = jax.vmap(conv_core, in_axes=(0, 0, None, None, None))
    finish_batch = jax.vmap(add_incoming)
    ahead_out, ahead_back = jax.vjp(core_batch, ahead_in, dt_raw, filters, a_log, dt_bias)
    behind_out, behind_back = jax.vjp(
        core_batch, behind, jnp.flip(dt_raw, axis=1), filters, a_log, dt_bias
    )
    ahead_state = pass_upward((ahead_out[1], ahead_out[2]))
    behind_state = pass_downward((behind_out[1], behind_out[2]))
    y_ahead, ahead_finish = jax.vjp(
        finish_batch, ahead_out[0], ahead_out[3], ahead_out[4], ahead_state
    )
    y_behind, behind_finish = jax.vjp(
        finish_batch, behind_out[0], behind_out[3], behind_out[4], behind_state
    )
    result = (y_ahead + jnp.flip(y_behind, axis=1)).astype(jnp.bfloat16)
    upstream = cotangent.astype(jnp.float32)
    grad_ahead = ahead_finish(upstream)
    grad_behind = behind_finish(jnp.flip(upstream, axis=1))
    later_ahead = pass_downward((ahead_out[1], grad_ahead[3]))
    later_behind = pass_upward((behind_out[1], grad_behind[3]))
    core_ahead = ahead_back(
        (
            grad_ahead[0],
            jnp.sum(later_ahead * ahead_state, axis=(-2, -1)),
            later_ahead,
            grad_ahead[1],
            grad_ahead[2],
        )
    )
    core_behind = behind_back(
        (
            grad_behind[0],
            jnp.sum(later_behind * behind_state, axis=(-2, -1)),
            later_behind,
            grad_behind[1],
            grad_behind[2],
        )
    )
    grad_padded = jnp.pad(core_ahead[0], ((0, 0), (0, margin), (0, 0))) + jnp.pad(
        jnp.flip(core_behind[0], axis=1), ((0, 0), (margin, 0), (0, 0))
    )
    rims = jnp.concatenate([grad_padded[:, :margin], grad_padded[:, length + margin :]], axis=1)
    rims = extended(rims.astype(jnp.bfloat16), (("seq", 1),), margin).astype(rims.dtype)
    own_rows = grad_padded[:, margin : length + margin]
    own_rows = own_rows.at[:, :margin].add(rims[:, :margin])
    own_rows = own_rows.at[:, length - margin :].add(rims[:, 3 * margin :])
    grad_inner = own_rows.astype(jnp.bfloat16)
    grad_dt = core_ahead[1] + jnp.flip(core_behind[1], axis=1)
    grad_projected = jnp.concatenate(
        [grad_inner[..., WIDTH:], grad_dt.astype(jnp.bfloat16)], axis=2
    )
    grad_weight = jnp.einsum(
        "std,stc->dc", tokens, grad_projected, preferred_element_type=jnp.float32
    )
    back_proj = jnp.einsum(
        "stc,dc->std", grad_projected, w_full, preferred_element_type=jnp.float32
    )
    grad_tokens = (grad_inner[..., :WIDTH].astype(jnp.float32) + back_proj).astype(jnp.bfloat16)
    grad_filters = core_ahead[2] + core_behind[2]
    grad_decay = jnp.stack([core_ahead[3] + core_behind[3], core_ahead[4] + core_behind[4]])
    return (result, grad_tokens, grad_weight, grad_filters, grad_decay)


def per_device(hidden, grad_out, w_proj, conv_w, a_log, dt_bias):
    w_full, conv_full = (
        lax.all_gather(w_proj, "zero", axis=0, tiled=True),
        lax.all_gather(conv_w, "zero", axis=1, tiled=True),
    )
    filters = conv_full.astype(jnp.float32)
    first = strand_pass(hidden, grad_out, w_full, filters, a_log, dt_bias)
    second = strand_pass(
        jnp.flip(hidden, axis=2), jnp.flip(grad_out, axis=2), w_full, filters, a_log, dt_bias
    )
    first_out, first_grad = (first[0], first[1])
    other_out = jnp.flip(second[0], axis=2)
    other_grad = jnp.flip(second[1], axis=2)
    grad_weight = first[2] + second[2]
    grad_filters = first[3] + second[3]
    grad_decay = first[4] + second[4]
    output = (first_out.astype(jnp.float32) + other_out.astype(jnp.float32)).astype(jnp.bfloat16)
    grad_hidden = (first_grad.astype(jnp.float32) + other_grad.astype(jnp.float32)).astype(
        jnp.bfloat16
    )
    part_weight, part_filters = (
        lax.psum_scatter(
            grad_weight.astype(jnp.bfloat16), "zero", scatter_dimension=0, tiled=True
        ).astype(jnp.float32),
        lax.psum_scatter(
            grad_filters.astype(jnp.bfloat16), "zero", scatter_dimension=1, tiled=True
        ).astype(jnp.float32),
    )
    share_weight, share_filters = (
        lax.psum(part_weight.astype(jnp.bfloat16), "seq").astype(jnp.float32),
        lax.psum(part_filters.astype(jnp.bfloat16), "seq").astype(jnp.float32),
    )
    grad_heads = lax.psum(grad_decay, ("seq", "zero"))
    return (output, grad_hidden, share_weight, share_filters, grad_heads)


def solution(mesh):
    return jax.shard_map(
        per_device,
        mesh=mesh,
        in_specs=(
            P(("grp", "zero"), "seq", None),
            P(("grp", "zero"), "seq", None),
            P("zero", None),
            P(None, "zero"),
            P(),
            P(),
        ),
        out_specs=(
            P(("grp", "zero"), "seq", None),
            P(("grp", "zero"), "seq", None),
            P(("grp", "zero"), None),
            P("grp", "zero"),
            P("grp", None),
        ),
        check_vma=False,
    )
```

profile of v0, /device:TPU:0, one launch (start us, length us, event | category | flops | bytes accessed | tf_op | source)
XLA Modules:
  0.0 792.8 jit_solution(859587964172044816)
XLA Ops:
  7.2 8.7 %all-gather.13 = bf16[4,320,148]{1,2,0:T(8,128)(2,1)S(1)} all-gather(bf16[1,320,148]{1,2,0:T(8,128)(2,1)} %bitcast.1260), channel_id=1, replica_groups=mesh['grp'=2,'seq'=4,'zero'=4] {'zero'}, dimensions={0}, use_global_device_ids=true | all-gather | bytes 473600 | tf_op jit(solution)/shard_map/all_gather | solution.py:195
  62.5 9.1 %all-gather.6 = bf16[4,1,20,1]{2,3,1,0:T(2,128)(2,1)} all-gather(bf16[1,1,20,1]{2,3,1,0:T(2,128)(2,1)S(1)} %get-tuple-element.1334), channel_id=8, replica_groups=mesh['grp'=2,'seq'=4,'zero'=4] {'seq'}, dimensions={0}, use_global_device_ids=true | all-gather | bytes 200 | tf_op jit(solution)/shard_map/all_gather | solution.py:18
  71.6 8.6 %all-gather.4 = bf16[4,1,20,1]{2,3,1,0:T(2,128)(2,1)} all-gather(bf16[1,1,20,1]{2,3,1,0:T(2,128)(2,1)S(1)} %get-tuple-element.1331), channel_id=6, replica_groups=mesh['grp'=2,'seq'=4,'zero'=4] {'seq'}, dimensions={0}, use_global_device_ids=true | all-gather | bytes 200 | tf_op jit(solution)/shard_map/all_gather | solution.py:18
  80.2 8.9 %all-gather.2 = bf16[4,1,20,1]{2,3,1,0:T(2,128)(2,1)} all-gather(bf16[1,1,20,1]{2,3,1,0:T(2,128)(2,1)S(1)} %get-tuple-element.1328), channel_id=4, replica_groups=mesh['grp'=2,'seq'=4,'zero'=4] {'seq'}, dimensions={0}, use_global_device_ids=true | all-gather | bytes 200 | tf_op jit(solution)/shard_map/all_gather | solution.py:18
  89.2 8.9 %all-gather = bf16[4,1,20,1]{2,3,1,0:T(2,128)(2,1)} all-gather(bf16[1,1,20,1]{2,3,1,0:T(2,128)(2,1)S(1)} %get-tuple-element.1325), channel_id=2, replica_groups=mesh['grp'=2,'seq'=4,'zero'=4] {'seq'}, dimensions={0}, use_global_device_ids=true | all-gather | bytes 200 | tf_op jit(solution)/shard_map/all_gather | solution.py:18
  102.7 6.6 slice.395
  109.3 6.6 slice.393
  137.2 6.6 slice.372
  143.8 6.6 slice.370
  150.4 6.6 slice.368
  157.0 6.6 slice.366
  174.2 19.9 %all-gather.7 = bf16[80,64,64]{2,1,0:T(8,128)(2,1)} all-gather(bf16[20,64,64]{2,1,0:T(8,128)(2,1)S(1)} %fusion.28), channel_id=9, replica_groups=mesh['grp'=2,'seq'=4,'zero'=4] {'seq'}, dimensions={0}, use_global_device_ids=true | all-gather | bytes 819200 | tf_op jit(solution)/shard_map/all_gather | solution.py:18
  203.9 19.0 %all-gather.11 = bf16[4,20,64,64]{3,2,1,0:T(8,128)(2,1)} all-gather(bf16[1,20,64,64]{3,2,1,0:T(8,128)(2,1)} %copy.689), channel_id=13, replica_groups=mesh['grp'=2,'seq'=4,'zero'=4] {'seq'}, dimensions={0}, use_global_device_ids=true | all-gather | bytes 819200 | tf_op jit(solution)/shard_map/all_gather | solution.py:18
  239.3 24.0 %all-gather.3 = bf16[80,64,64]{2,1,0:T(8,128)(2,1)} all-gather(bf16[20,64,64]{2,1,0:T(8,128)(2,1)S(1)} %fusion.26), channel_id=5, replica_groups=mesh['grp'=2,'seq'=4,'zero'=4] {'seq'}, dimensions={0}, use_global_device_ids=true | all-gather | bytes 819200 | tf_op jit(solution)/shard_map/all_gather | solution.py:18
  264.2 8.3 %while.69 = (s32[]{:T(128)}, f32[1,20,64,64]{3,2,1,0:T(8,128)}, s32[]{:T(128)}, bf16[4,1,20]{2,1,0:T(2,128)(2,1)}, bf16[4,1,20,64,64]{4,3,2,1,0:T(8,128)(2,1)}, ...) while((s32[]{:T(128)}, f32[1,20,64,64]{3,2,1,0:T(8,128)}, s32[]{:T(128)}, bf16[4,1,20]{2,1,0:T(2,128)(2,1)}, ...), condition=%wide.region_5.7_spmd, body=%wide.region_4.6_spmd.sunk | while | flops 245786 | bytes 819555 | solution.py:35
  276.5 19.0 %all-gather.9 = bf16[4,20,64,64]{3,2,1,0:T(8,128)(2,1)} all-gather(bf16[1,20,64,64]{3,2,1,0:T(8,128)(2,1)} %copy.664), channel_id=11, replica_groups=mesh['grp'=2,'seq'=4,'zero'=4] {'seq'}, dimensions={0}, use_global_device_ids=true | all-gather | bytes 819200 | tf_op jit(solution)/shard_map/all_gather | solution.py:18
  340.2 29.1 %all-gather.10 = bf16[4,20,64,64]{3,2,1,0:T(8,128)(2,1)} all-gather(bf16[1,20,64,64]{3,2,1,0:T(8,128)(2,1)} %copy.684), channel_id=12, replica_groups=mesh['grp'=2,'seq'=4,'zero'=4] {'seq'}, dimensions={0}, use_global_device_ids=true | all-gather | bytes 819200 | tf_op jit(solution)/shard_map/all_gather | solution.py:18
  370.3 8.5 %while.74 = (s32[]{:T(128)}, f32[1,20,64,64]{3,2,1,0:T(8,128)}, s32[]{:T(128)}, bf16[4,1,20]{2,1,0:T(2,128)(2,1)}, bf16[4,1,20,64,64]{4,3,2,1,0:T(8,128)(2,1)}, ...) while((s32[]{:T(128)}, f32[1,20,64,64]{3,2,1,0:T(8,128)}, s32[]{:T(128)}, bf16[4,1,20]{2,1,0:T(2,128)(2,1)}, ...), condition=%wide.region_44.46_spmd, body=%wide.region_43.45_spmd.sunk | while | flops 245786 | bytes 819555 | solution.py:35
  393.5 21.7 %all-gather.8 = bf16[4,20,64,64]{3,2,1,0:T(8,128)(2,1)} all-gather(bf16[1,20,64,64]{3,2,1,0:T(8,128)(2,1)} %copy.659), channel_id=10, replica_groups=mesh['grp'=2,'seq'=4,'zero'=4] {'seq'}, dimensions={0}, use_global_device_ids=true | all-gather | bytes 819200 | tf_op jit(solution)/shard_map/all_gather | solution.py:18
  416.1 8.3 %while.72 = (s32[]{:T(128)}, f32[1,20,64,64]{3,2,1,0:T(8,128)}, s32[]{:T(128)}, bf16[4,1,20]{2,1,0:T(2,128)(2,1)}, bf16[4,1,20,64,64]{4,3,2,1,0:T(8,128)(2,1)}, ...) while((s32[]{:T(128)}, f32[1,20,64,64]{3,2,1,0:T(8,128)}, s32[]{:T(128)}, bf16[4,1,20]{2,1,0:T(2,128)(2,1)}, ...), condition=%wide.region_14.16_spmd, body=%wide.region_13.15_spmd.sunk | while | flops 245786 | bytes 819555 | solution.py:35
  429.0 23.8 %all-gather.5 = bf16[80,64,64]{2,1,0:T(8,128)(2,1)} all-gather(bf16[20,64,64]{2,1,0:T(8,128)(2,1)S(1)} %fusion.27), channel_id=7, replica_groups=mesh['grp'=2,'seq'=4,'zero'=4] {'seq'}, dimensions={0}, use_global_device_ids=true | all-gather | bytes 819200 | tf_op jit(solution)/shard_map/all_gather | solution.py:18
  455.1 26.7 %all-gather.1 = bf16[80,64,64]{2,1,0:T(8,128)(2,1)} all-gather(bf16[20,64,64]{2,1,0:T(8,128)(2,1)S(1)} %fusion.25), channel_id=3, replica_groups=mesh['grp'=2,'seq'=4,'zero'=4] {'seq'}, dimensions={0}, use_global_device_ids=true | all-gather | bytes 819200 | tf_op jit(solution)/shard_map/all_gather | solution.py:18
  507.1 8.0 %reverse.8 = f32[1,256,1408]{1,2,0:T(8,128)} reverse(f32[1,256,1408]{1,2,0:T(8,128)S(1)} %bitcast.1187), dimensions={1} | reverse | bytes 2883584
  525.7 12.4 %reverse.9 = f32[1,256,1408]{1,2,0:T(8,128)} reverse(f32[1,256,1408]{1,2,0:T(8,128)} %bitcast.1188), dimensions={1} | reverse | bytes 2883584
  570.1 6.8 collective-permute-start.6
  592.5 6.2 collective-permute-start.4
  671.3 6.6 scatter-add.19
  686.8 6.6 scatter-add.15
  697.5 31.7 %psum.23 = f32[2,20]{1,0:T(2,128)} all-reduce(f32[2,20]{1,0:T(2,128)S(1)} %maximum_add_fusion), channel_id=1, replica_groups=mesh['grp'=2,'seq'=4,'zero'=4] {'seq','zero'}, use_global_device_ids=true, to_apply=%region_100.102 | all-reduce | flops 40 | bytes 320 | tf_op jit(solution)/shard_map/psum | solution.py:225
  735.0 12.3 %reduce-scatter.9.cloned.1.call-done = bf16[352,4]{1,0:T(8,128)(2,1)} async-done(((bf16[1408,4]{1,0:T(8,128)(2,1)}), bf16[352,4]{1,0:T(8,128)(2,1)}) %reduce-scatter.9.cloned.1.call-update) | async-done | bytes 2832
  748.3 11.7 %psum.22 = bf16[4,352]{1,0:T(4,128)(2,1)S(1)} all-reduce(bf16[4,352]{1,0:T(4,128)(2,1)S(1)} %copy.719), channel_id=1, replica_groups=mesh['grp'=2,'seq'=4,'zero'=4] {'seq'}, use_global_device_ids=true, to_apply=%region_91.93 | all-reduce | flops 1408 | bytes 5632 | tf_op jit(solution)/shard_map/psum | solution.py:223
  760.6 23.9 %all-reduce.58.cloned.1.call-done = bf16[320,148]{0,1:T(8,128)(2,1)} async-done(((bf16[320,148]{0,1:T(8,128)(2,1)}), bf16[320,148]{0,1:T(8,128)(2,1)}) %all-reduce.58.cloned.1.call-update) | async-done | bytes 94736 | tf_op jit(solution)/shard_map/psum | solution.py:222
  (850 shorter events, 387.9 us)
Async XLA Ops:
  7.2 724.8 %reduce-scatter.7.cloned.1.call-start = ((), (), s32[]{:S(2)}) async-start(), calls=%async_computation.3 | async-start | bytes 819200
  18.1 106.2 %collective-permute-start.1 = (bf16[1,3,1408]{1,2,0:T(8,128)(2,1)}, bf16[1,3,1408]{1,2,0:T(8,128)(2,1)}, u32[]{:S(2)}, u32[]{:S(2)}) collective-permute-start(bf16[1,3,1408]{1,2,0:T(8,128)(2,1)} %get-tuple-element.1305), channel_id=1, source_target_pairs={{4,0},{8,4},{12,8},{5,1},{9,5},{13,9},{6,2},{10,6},{14,10},{7,3},{... | collective-permute-start | bytes 25352 | tf_op jit(solution)/shard_map/ppermute | solution.py:46
  19.4 104.9 %collective-permute-start = (bf16[1,3,1408]{1,2,0:T(8,128)(2,1)}, bf16[1,3,1408]{1,2,0:T(8,128)(2,1)}, u32[]{:S(2)}, u32[]{:S(2)}) collective-permute-start(bf16[1,3,1408]{1,2,0:T(8,128)(2,1)} %get-tuple-element.1304), channel_id=1, source_target_pairs={{0,4},{4,8},{8,12},{1,5},{5,9},{9,13},{2,6},{6,10},{10,14},{3,7},{... | collective-permute-start | bytes 25352 | tf_op jit(solution)/shard_map/ppermute | solution.py:45
  25.1 73.0 %copy-start.25 = (bf16[1,128,1280]{1,2,0:T(8,128)(2,1)}, bf16[1,128,1280]{1,2,0:T(8,128)(2,1)S(1)}, u32[]{:S(2)}) copy-start(bf16[1,128,1280]{1,2,0:T(8,128)(2,1)S(1)} %rev.50) | copy-start | bytes 983044
  26.6 71.6 %collective-permute-start.3 = (bf16[1,3,1408]{1,2,0:T(8,128)(2,1)}, bf16[1,3,1408]{1,2,0:T(8,128)(2,1)}, u32[]{:S(2)}, u32[]{:S(2)}) collective-permute-start(bf16[1,3,1408]{1,2,0:T(8,128)(2,1)} %get-tuple-element.1307), channel_id=1, source_target_pairs={{4,0},{8,4},{12,8},{5,1},{9,5},{13,9},{6,2},{10,6},{14,10},{7,3},{... | collective-permute-start | bytes 25352 | tf_op jit(solution)/shard_map/ppermute | solution.py:46
  27.9 70.3 %collective-permute-start.2 = (bf16[1,3,1408]{1,2,0:T(8,128)(2,1)}, bf16[1,3,1408]{1,2,0:T(8,128)(2,1)}, u32[]{:S(2)}, u32[]{:S(2)}) collective-permute-start(bf16[1,3,1408]{1,2,0:T(8,128)(2,1)} %get-tuple-element.1306), channel_id=1, source_target_pairs={{0,4},{4,8},{8,12},{1,5},{5,9},{9,13},{2,6},{6,10},{10,14},{3,7},{... | collective-permute-start | bytes 25352 | tf_op jit(solution)/shard_map/ppermute | solution.py:45
  33.6 23.5 %copy-start.52 = (f32[1,1,128,20]{3,2,1,0:T(8,128)}, f32[1,1,128,20]{3,2,1,0:T(8,128)S(1)}, u32[]{:S(2)}) copy-start(f32[1,1,128,20]{3,2,1,0:T(8,128)S(1)} %reduce_window_sum.90) | copy-start | bytes 30724
  34.4 21.1 %copy-start.17 = (bf16[1,128,1280]{1,2,0:T(8,128)(2,1)}, bf16[1,128,1280]{1,2,0:T(8,128)(2,1)S(1)}, u32[]{:S(2)}) copy-start(bf16[1,128,1280]{1,2,0:T(8,128)(2,1)S(1)} %copy.656) | copy-start | bytes 983044
  35.8 24.7 %copy-start.54 = (f32[1,1,128,20]{3,2,1,0:T(8,128)}, f32[1,1,128,20]{3,2,1,0:T(8,128)S(1)}, u32[]{:S(2)}) copy-start(f32[1,1,128,20]{3,2,1,0:T(8,128)S(1)} %reduce_window_sum.86) | copy-start | bytes 30724
  37.2 21.9 %copy-start.56 = (f32[1,1,128,20]{3,2,1,0:T(8,128)}, f32[1,1,128,20]{3,2,1,0:T(8,128)S(1)}, u32[]{:S(2)}) copy-start(f32[1,1,128,20]{3,2,1,0:T(8,128)S(1)} %reduce_window_sum.88) | copy-start | bytes 30724
  38.6 22.6 %copy-start.58 = (f32[1,1,128,20]{3,2,1,0:T(8,128)}, f32[1,1,128,20]{3,2,1,0:T(8,128)S(1)}, u32[]{:S(2)}) copy-start(f32[1,1,128,20]{3,2,1,0:T(8,128)S(1)} %reduce_window_sum.84) | copy-start | bytes 30724
  45.0 80.9 %copy-start.140 = (f32[1408]{0:T(1024)}, f32[1408]{0:T(1024)S(1)}, u32[]{:S(2)}) copy-start(f32[1408]{0:T(1024)S(1)} %get-tuple-element.1150) | copy-start | bytes 16900
  45.1 80.9 %copy-start.142 = (f32[1408]{0:T(1024)}, f32[1408]{0:T(1024)S(1)}, u32[]{:S(2)}) copy-start(f32[1408]{0:T(1024)S(1)} %get-tuple-element.1151) | copy-start | bytes 16900
  199.6 23.3 %copy-start.2 = (f32[1,20,64,64]{3,2,1,0:T(8,128)}, f32[1,20,64,64]{3,2,1,0:T(8,128)S(1)}, u32[]{:S(2)}) copy-start(f32[1,20,64,64]{3,2,1,0:T(8,128)S(1)} %get-tuple-element.760) | copy-start | bytes 983044
  568.8 93.1 %collective-permute-start.7 = (bf16[1,3,1408]{1,2,0:T(8,128)(2,1)}, bf16[1,3,1408]{1,2,0:T(8,128)(2,1)}, u32[]{:S(2)}, u32[]{:S(2)}) collective-permute-start(bf16[1,3,1408]{1,2,0:T(8,128)(2,1)} %get-tuple-element.1271), channel_id=1, source_target_pairs={{4,0},{8,4},{12,8},{5,1},{9,5},{13,9},{6,2},{10,6},{14,10},{7,3},{... | collective-permute-start | bytes 25352 | tf_op jit(solution)/shard_map/ppermute | solution.py:46
  570.1 91.8 %collective-permute-start.6 = (bf16[1,3,1408]{1,2,0:T(8,128)(2,1)}, bf16[1,3,1408]{1,2,0:T(8,128)(2,1)}, u32[]{:S(2)}, u32[]{:S(2)}) collective-permute-start(bf16[1,3,1408]{1,2,0:T(8,128)(2,1)} %get-tuple-element.1270), channel_id=1, source_target_pairs={{0,4},{4,8},{8,12},{1,5},{5,9},{9,13},{2,6},{6,10},{10,14},{3,7},{... | collective-permute-start | bytes 25352 | tf_op jit(solution)/shard_map/ppermute | solution.py:45
  585.5 21.2 %copy-start.117 = (f32[20,128]{0,1:T(8,128)}, f32[20,128]{0,1:T(8,128)S(1)}, u32[]{:S(2)}) copy-start(f32[20,128]{0,1:T(8,128)S(1)} %copy.668) | copy-start | bytes 30724
  587.1 21.4 %copy-start.55 = (f32[1,1,128,20]{3,2,1,0:T(8,128)S(1)}, f32[1,1,128,20]{3,2,1,0:T(8,128)}, u32[]{:S(2)}) copy-start(f32[1,1,128,20]{3,2,1,0:T(8,128)} %copy-done.54) | copy-start | bytes 30724
  587.1 21.4 %copy-start.61 = (f32[1,128,20]{2,1,0:T(8,128)S(1)}, f32[1,128,20]{2,1,0:T(8,128)}, u32[]{:S(2)}) copy-start(f32[1,128,20]{2,1,0:T(8,128)} %copy-done.60) | copy-start | bytes 30724
  587.1 21.4 %copy-start.119 = (f32[20,128]{0,1:T(8,128)S(1)}, f32[20,128]{0,1:T(8,128)}, u32[]{:S(2)}) copy-start(f32[20,128]{0,1:T(8,128)} %copy.674) | copy-start | bytes 30724
  587.1 21.4 %copy-start.134 = (f32[20,128]{0,1:T(8,128)S(1)}, f32[20,128]{0,1:T(8,128)}, u32[]{:S(2)}) copy-start(f32[20,128]{0,1:T(8,128)} %copy.675) | copy-start | bytes 30724
  587.2 21.4 %copy-start.214 = (f32[20]{0:T(128)S(1)}, f32[20]{0:T(128)}, u32[]{:S(2)}) copy-start(f32[20]{0:T(128)} %copy-done.213) | copy-start | bytes 244
  587.2 21.4 %copy-start.216 = (f32[20]{0:T(128)S(1)}, f32[20]{0:T(128)}, u32[]{:S(2)}) copy-start(f32[20]{0:T(128)} %get-tuple-element.1329) | copy-start | bytes 244
  589.2 21.5 %copy-start.123 = (f32[1,1,128,20]{3,2,1,0:T(8,128)}, f32[1,1,128,20]{3,2,1,0:T(8,128)S(1)}, u32[]{:S(2)}) copy-start(f32[1,1,128,20]{3,2,1,0:T(8,128)S(1)} %reduce_window_sum.95) | copy-start | bytes 30724
  591.2 86.8 %collective-permute-start.5 = (bf16[1,3,1408]{1,2,0:T(8,128)(2,1)}, bf16[1,3,1408]{1,2,0:T(8,128)(2,1)}, u32[]{:S(2)}, u32[]{:S(2)}) collective-permute-start(bf16[1,3,1408]{1,2,0:T(8,128)(2,1)} %get-tuple-element.1269), channel_id=1, source_target_pairs={{4,0},{8,4},{12,8},{5,1},{9,5},{13,9},{6,2},{10,6},{14,10},{7,3},{... | collective-permute-start | bytes 25352 | tf_op jit(solution)/shard_map/ppermute | solution.py:46
  592.5 85.5 %collective-permute-start.4 = (bf16[1,3,1408]{1,2,0:T(8,128)(2,1)}, bf16[1,3,1408]{1,2,0:T(8,128)(2,1)}, u32[]{:S(2)}, u32[]{:S(2)}) collective-permute-start(bf16[1,3,1408]{1,2,0:T(8,128)(2,1)} %get-tuple-element.1268), channel_id=1, source_target_pairs={{0,4},{4,8},{8,12},{1,5},{5,9},{9,13},{2,6},{6,10},{10,14},{3,7},{... | collective-permute-start | bytes 25352 | tf_op jit(solution)/shard_map/ppermute | solution.py:45
  639.3 24.9 %copy-start.14 = (f32[1,131,1408]{1,2,0:T(8,128)S(1)}, f32[1,131,1408]{1,2,0:T(8,128)}, u32[]{:S(2)}) copy-start(f32[1,131,1408]{1,2,0:T(8,128)} %copy-done.13) | copy-start | bytes 2213380
  695.0 34.3 %copy-start.88 = (f32[1,128,1280]{2,1,0:T(8,128)S(1)}, f32[1,128,1280]{2,1,0:T(8,128)}, u32[]{:S(2)}) copy-start(f32[1,128,1280]{2,1,0:T(8,128)} %rev.49) | copy-start | bytes 1966084
  695.0 34.3 %copy-start.89 = (f32[1,128,1280]{2,1,0:T(8,128)S(1)}, f32[1,128,1280]{2,1,0:T(8,128)}, u32[]{:S(2)}) copy-start(f32[1,128,1280]{2,1,0:T(8,128)} %copy.618) | copy-start | bytes 1966084
  695.0 34.3 %copy-start.90 = (f32[1,128,1280]{2,1,0:T(8,128)S(1)}, f32[1,128,1280]{2,1,0:T(8,128)}, u32[]{:S(2)}) copy-start(f32[1,128,1280]{2,1,0:T(8,128)} %copy.619) | copy-start | bytes 1966084
  696.1 51.2 %reduce-scatter.9.cloned.1.call-start = ((), (), s32[]{:S(2)}) async-start(), calls=%async_computation.4 | async-start | bytes 450560
  729.2 55.2 %all-reduce.58.cloned.1.call-start = ((), (), s32[]{:S(2)}) async-start(), calls=%async_computation.2 | async-start | bytes 233472 | tf_op jit(solution)/shard_map/psum | solution.py:222
  (238 other events, 1134.9 us)
Sparse Core Ops, SparseCore 0:
  696.3 26.8 reduce-scatter.6
  729.4 17.9 reduce-scatter.8
  750.3 34.0 all-reduce.57
where the time goes:
time: 808 us; the launch traced here: 793 us
  blocking collectives  276 us (34%)
  local copies, waits for them, and re-layouts  219 us (27%)
  other arithmetic  139 us (17%)
  matrix products  75.8 us (9%)
  waiting for transfers between devices  36.3 us (4%)
  starting transfers between devices  28.9 us (4%)
  between operations  17 us (2%)
    all_gather x12, blocking collectives, prefix(): lax.all_gather(a.astype(kind), axis)  219 us
    unnamed x530, local copies, waits for them, and re-layouts  38.1 us
    slice x6, local copies, waits for them, and re-layouts, conv_core(): ahead_in[KERNEL - 1 - step_back:KERNEL - 1 - step_back + length]  37.1 us
    psum x1, blocking collectives, per_device(): grad_heads = lax.psum(grad_decay, ('seq', 'zero'))  31.7 us
    psum x1, waiting for transfers between devices, per_device(): lax.psum(part_weight.astype(jnp.bfloat16), 'seq').astype(jnp.float32)  23.9 us
    ppermute x4, starting transfers between devices, extended(): before = lax.ppermute(last, axis, up)  23.6 us
    add x12, other arithmetic, combine_states(): later[0][..., None, None] * earlier[1] + later[1]  22.9 us
    dot_general x12, matrix products, conv_core(): jnp.einsum('khij,kjhp->kihp', weights, values, preferred_element_type=jnp...  20.9 us
  transfers between devices with their start and end apart: 11, of which 2 were waited for; matrix products, arithmetic and copies ran while one was open for 19% of the time, Pallas kernels for 0%

commit v1 on v0

v1 whole, which is shorter than its diff:
```python
import functools
import jax
import jax.numpy as jnp
from jax import lax
from jax.experimental import pallas as pl
from jax.experimental.pallas import tpu as pltpu
from jax.sharding import PartitionSpec as P

WIDTH = 1280
STATE = 64
HEAD_DIM = 64
SPAN = 128
KERNEL = 4
HEADS = 20
PAIRS = WIDTH // 128
CHANNELS = WIDTH + 2 * STATE
EDGE = 8
EXT = SPAN + 2 * EDGE
F32 = jnp.float32
BF16 = jnp.bfloat16
LOW = -1e30
COMBOS = ((0, 0), (0, 1), (1, 0), (1, 1))


def mm(a, b):
    return jnp.dot(a, b, preferred_element_type=F32)


def mm_nt(a, b):
    return lax.dot_general(a, b, (((1,), (1,)), ((), ())), preferred_element_type=F32)


def mm_tn(a, b):
    return lax.dot_general(a, b, (((0,), (0,)), ((), ())), preferred_element_type=F32)


def exact(a, b):
    return jnp.dot(a, b, preferred_element_type=F32, precision=lax.Precision.HIGHEST)


def iota(dim, shape=(128, 128)):
    return lax.broadcasted_iota(jnp.int32, shape, dim)


def mirror(dtype=BF16):
    return jnp.where(iota(0) + iota(1) == 127, 1.0, 0.0).astype(dtype)


def col(x, h):
    return jnp.sum(jnp.where(iota(1) == h, x, 0.0), axis=1, keepdims=True)


def softplus(x):
    return jnp.maximum(x, 0.0) + jnp.log1p(jnp.exp(-jnp.abs(x)))


def sigmoid(x):
    return 1.0 / (1.0 + jnp.exp(-x))


def head_of(strand, pair, r):
    return 2 * pair + r if strand == 0 else HEADS - 1 - 2 * pair - r


def shifted(x):
    back = [x[EDGE : EDGE + SPAN]]
    fore = [back[0]]
    for k in range(1, KERNEL):
        back.append(pltpu.roll(x, k, 0)[EDGE : EDGE + SPAN])
        fore.append(pltpu.roll(x, EXT - k, 0)[EDGE : EDGE + SPAN])
    return back, fore


def conv(taps, rows):
    out = taps[0:1] * rows[0]
    for k in range(1, KERNEL):
        out = out + taps[k : k + 1] * rows[k]
    return out


def conv_back(taps, dm, direction):
    zero = jnp.zeros((EDGE, 128), F32)
    wide = jnp.concatenate([zero, dm, zero], axis=0)
    out = taps[0:1] * wide
    for k in range(1, KERNEL):
        out = out + taps[k : k + 1] * pltpu.roll(wide, EXT - k if direction == 0 else k, 0)
    return out


def tap_grads(dm, rows):
    parts = [jnp.sum(dm * rows[k], axis=0, keepdims=True) for k in range(KERNEL)]
    return jnp.concatenate(parts + [jnp.zeros((8 - KERNEL, 128), F32)], axis=0)


def last_row(x, direction):
    return x[SPAN - 1 : SPAN] if direction == 0 else x[0:1]


def lanes(i):
    return pl.ds(pl.multiple_of(i * 128, 128), 128)


def first_kernel(
    x_ref, go_ref, w_ref, f_ref, alog_ref, bias_ref,
    state_ref, gstate_ref, dec_ref, wr_ref, bcx_ref, dtx_ref, within_ref,
    tow_t, e_col, bc_t,
):
    flip = mirror()
    for b in range(PAIRS):
        wr_ref[b * 128 : (b + 1) * 128] = mm(
            flip, w_ref[(PAIRS - 1 - b) * 128 : (PAIRS - b) * 128]
        ).astype(BF16)
    x_all = x_ref[...]
    rate = jnp.exp(alog_ref[...])
    for s in range(2):
        proj = mm(x_all, w_ref[...] if s == 0 else wr_ref[...])
        bcx = proj[:, :128].astype(BF16).astype(F32)
        bcx_ref[s] = bcx
        dtx = proj[EDGE : EDGE + SPAN, 128:] + bias_ref[...]
        dtx_ref[s] = dtx
        delta = softplus(dtx)
        rows = shifted(bcx)
        for d in range(2):
            c = 2 * s + d
            tri = iota(0) >= iota(1) if d == 0 else iota(0) <= iota(1)
            within = exact(jnp.where(tri, 1.0, 0.0), -rate * delta)
            within_ref[c] = within
            mixed = conv(f_ref[:, WIDTH:], rows[d])
            act = (mixed * sigmoid(mixed)).astype(BF16).astype(F32)
            bc_t[c] = act.T
            tow_t[c] = (jnp.exp(last_row(within, d) - within) * delta).T
            e_col[c] = jnp.exp(within)
            dec_ref[c] = jnp.zeros((16, 128), F32)

    def pair_step(i, carry):
        x = x_ref[:, lanes(i)].astype(F32)
        g = go_ref[:, lanes(i)].astype(F32)
        rows = shifted(x)
        taps = (
            f_ref[:, lanes(i)],
            mm(f_ref[:, lanes(PAIRS - 1 - i)].astype(BF16), flip),
        )
        low = iota(1) < HEAD_DIM
        low_half = iota(1, (STATE, 128)) < HEAD_DIM
        for s, d in COMBOS:
            c = 2 * s + d
            mixed = conv(taps[s], rows[d])
            values = (mixed * sigmoid(mixed)).astype(BF16)
            heads = [head_of(s, i, r) for r in range(2)]
            b_t = bc_t[c, 0:STATE]
            bw = jnp.concatenate(
                [b_t * tow_t[c, pl.ds(h, 1), :] for h in heads], axis=0
            ).astype(BF16)
            st = mm(bw, values)
            state_ref[c, i] = jnp.where(low_half, st[:STATE], st[STATE:])
            e = e_col[c]
            e0, e1 = [col(e, h) for h in heads]
            e_pair = jnp.where(low, e0, e1)
            gstate_ref[c, i] = mm(bc_t[c, STATE:128].astype(BF16), (e_pair * g).astype(BF16))
            dec_ref[c, pl.ds(i, 1), :] = last_row(e_pair, d)
        return carry

    lax.fori_loop(0, PAIRS, pair_step, 0)


def main_kernel(
    x_ref, go_ref, f_ref, alog_ref, bcx_ref, dtx_ref, within_ref, sin_ref, gin_ref,
    out_ref, gi_ref, gf_ref, ddt_ref, heads_ref,
    e_col, f_col, tow, within_t, delta_t, score, d_score, d_b, d_c, d_l, d_lt, d_dc, d_dt, bc_act,
):
    flip = mirror()
    rate = jnp.exp(alog_ref[...])
    for s in range(2):
        delta = softplus(dtx_ref[s])
        delta_t[s] = delta.T
        rows = shifted(bcx_ref[s])
        d_dc[s] = jnp.zeros((128, 128), F32)
        d_dt[s] = jnp.zeros((128, 128), F32)
        for d in range(2):
            c = 2 * s + d
            within = within_ref[c]
            within_t[c] = within.T
            e_col[c] = jnp.exp(within)
            f = jnp.exp(last_row(within, d) - within)
            f_col[c] = f
            tow[c] = f * delta
            mixed = conv(f_ref[:, WIDTH:], rows[d])
            act = (mixed * sigmoid(mixed)).astype(BF16)
            bc_act[c, 0] = act[:, :STATE].astype(F32)
            bc_act[c, 1] = act[:, STATE:].astype(F32)
            score[c] = mm_nt(act[:, STATE:], act[:, :STATE])
            d_score[c] = jnp.zeros((128, 128), F32)
            d_l[c] = jnp.zeros((128, 128), F32)
            d_lt[c] = jnp.zeros((128, 128), F32)
            d_b[c] = jnp.zeros((128, STATE), F32)
            d_c[c] = jnp.zeros((128, STATE), F32)

    def pair_step(i, carry):
        x = x_ref[:, lanes(i)].astype(F32)
        go = go_ref[:, lanes(i)]
        g = go.astype(F32)
        rows = shifted(x)
        taps = (
            f_ref[:, lanes(i)],
            mm(f_ref[:, lanes(PAIRS - 1 - i)].astype(BF16), flip),
        )
        lane = iota(1)
        low = lane < HEAD_DIM
        low_half = iota(1, (STATE, 128)) < HEAD_DIM
        none = jnp.zeros((128, 128), BF16)
        g_two = jnp.concatenate([jnp.where(low, go, none), jnp.where(low, none, go)], axis=0)
        strands = []
        for s in range(2):
            y = jnp.zeros((128, 128), F32)
            gi = jnp.zeros((EXT, 128), F32)
            gf = jnp.zeros((8, 128), F32)
            heads = [head_of(s, i, r) for r in range(2)]
            delta_r = [delta_t[s, pl.ds(h, 1), :] for h in heads]
            for d in range(2):
                c = 2 * s + d
                end = SPAN - 1 if d == 0 else 0
                keep = iota(0) >= lane if d == 0 else iota(0) <= lane
                mixed = conv(taps[s], rows[d])
                sig = sigmoid(mixed)
                values = (mixed * sig).astype(BF16)
                b_mat, c_mat = bc_act[c, 0], bc_act[c, 1]
                within = within_ref[c]
                e_all, f_all, tow_all = e_col[c], f_col[c], tow[c]
                sc = score[c]
                decays, sds, ws, tows, fs, es = [], [], [], [], [], []
                for r, h in enumerate(heads):
                    gap = jnp.where(keep, col(within, h) - within_t[c, pl.ds(h, 1), :], LOW)
                    decay = jnp.exp(gap)
                    decays.append(decay)
                    sds.append(sc * decay)
                    ws.append((sds[r] * delta_r[r]).astype(BF16))
                    tows.append(col(tow_all, h))
                    fs.append(col(f_all, h))
                    es.append(col(e_all, h))
                e_pair = jnp.where(low, es[0], es[1])
                ge = (e_pair * g).astype(BF16)
                s_in, g_in = sin_ref[c, i], gin_ref[c, i]
                y_two = mm(jnp.concatenate(ws, axis=0), values)
                inter = mm(c_mat.astype(BF16), s_in) * e_pair
                y = y + jnp.where(low, y_two[:128], y_two[128:]) + inter
                d_w = mm_nt(g_two, values)
                bws = jnp.concatenate([(t * b_mat).astype(BF16) for t in tows], axis=0)
                dv_state = mm(bws, g_in)
                dv = jnp.where(
                    low,
                    mm_tn(ws[0], go) + dv_state[:128],
                    mm_tn(ws[1], go) + dv_state[128:],
                )
                v_two = jnp.concatenate(
                    [jnp.where(low, values, none), jnp.where(low, none, values)], axis=0
                )
                d_bw = mm_nt(v_two, g_in)
                d_c[c] += mm_nt(ge, s_in)
                q = g * inter
                both = jnp.sum(g_in.astype(F32) * s_in.astype(F32), axis=0, keepdims=True)
                ends = both * last_row(e_pair, d)
                low_row = iota(1, (1, 128)) < HEAD_DIM
                ds = d_score[c]
                db = d_b[c]
                dl = d_l[c]
                dd = d_dc[s]
                for r, h in enumerate(heads):
                    mine = low if r == 0 else ~low
                    mine_row = low_row if r == 0 else ~low_row
                    dw = d_w[128 * r : 128 * r + 128]
                    rr = dw * sds[r]
                    rows_sum = jnp.sum(rr * delta_r[r], axis=1, keepdims=True)
                    cols_sum = jnp.sum(rr, axis=0, keepdims=True)
                    d_dt[s, pl.ds(h, 1), :] += cols_sum
                    d_lt[c, pl.ds(h, 1), :] -= cols_sum * delta_r[r]
                    ds = ds + dw * decays[r] * delta_r[r]
                    dbw = d_bw[128 * r : 128 * r + 128]
                    d_tow = jnp.sum(dbw * b_mat, axis=1, keepdims=True)
                    db = db + tows[r] * dbw
                    dd = dd + jnp.where(lane == h, d_tow * fs[r], 0.0)
                    t = d_tow * tows[r]
                    total = jnp.sum(t, axis=0, keepdims=True) + jnp.sum(
                        jnp.where(mine_row, ends, 0.0), axis=1, keepdims=True
                    )
                    q_sum = jnp.sum(jnp.where(mine, q, 0.0), axis=1, keepdims=True)
                    at_end = jnp.where(iota(0, (128, 1)) == end, total, 0.0)
                    dl = dl + jnp.where(lane == h, rows_sum - t + q_sum + at_end, 0.0)
                d_score[c] = ds
                d_b[c] = db
                d_l[c] = dl
                d_dc[s] = dd
                dact = dv.astype(BF16).astype(F32)
                dm = dact * (sig * (1.0 + mixed * (1.0 - sig)))
                gf = gf + tap_grads(dm, rows[d])
                gi = gi + conv_back(taps[s], dm, d)
            strands.append(y.astype(BF16).astype(F32))
            gi_ref[s, :, lanes(i)] = gi
            gf_ref[s, :, lanes(i)] = gf
        out_ref[:, lanes(i)] = (strands[0] + strands[1]).astype(BF16)
        return carry

    lax.fori_loop(0, PAIRS, pair_step, 0)

    d_alog = jnp.zeros((1, 128), F32)
    d_bias = jnp.zeros((1, 128), F32)
    for s in range(2):
        rows = shifted(bcx_ref[s])
        dtx = dtx_ref[s]
        log_decay = -rate * softplus(dtx)
        d_delta = d_dc[s] + d_dt[s].T
        gi = jnp.zeros((EXT, 128), F32)
        gf = jnp.zeros((8, 128), F32)
        taps = f_ref[:, WIDTH:]
        for d in range(2):
            c = 2 * s + d
            tri = iota(0) <= iota(1) if d == 0 else iota(0) >= iota(1)
            d_log = exact(jnp.where(tri, 1.0, 0.0), d_l[c] + d_lt[c].T)
            d_delta = d_delta - rate * d_log
            d_alog = d_alog + jnp.sum(d_log * log_decay, axis=0, keepdims=True)
            ds = d_score[c].astype(BF16)
            dc = d_c[c] + mm(ds, bc_act[c, 0].astype(BF16))
            db = d_b[c] + mm_tn(ds, bc_act[c, 1].astype(BF16))
            dact = jnp.concatenate([db, dc], axis=1).astype(BF16).astype(F32)
            mixed = conv(taps, rows[d])
            sig = sigmoid(mixed)
            dm = dact * (sig * (1.0 + mixed * (1.0 - sig)))
            gf = gf + tap_grads(dm, rows[d])
            gi = gi + conv_back(taps, dm, d)
        d_raw = d_delta * sigmoid(dtx)
        ddt_ref[s] = d_raw.astype(BF16)
        d_bias = d_bias + jnp.sum(d_raw, axis=0, keepdims=True)
        gi_ref[s, :, WIDTH:] = gi
        gf_ref[s, :, WIDTH:] = gf
    heads_ref[...] = jnp.concatenate([d_alog, d_bias, jnp.zeros((6, 128), F32)], axis=0)


def last_kernel(
    hid_ref, w_ref, wr_ref, gi_ref, before_ref, after_ref, ddt_ref, gf_ref,
    gh_ref, gw_ref, gc_ref,
):
    flip = mirror()

    def own(s, at):
        top = gi_ref[s, EDGE : 2 * EDGE, at] + before_ref[s, :, at].astype(F32)
        low = gi_ref[s, SPAN : SPAN + EDGE, at] + after_ref[s, :, at].astype(F32)
        return jnp.concatenate([top, gi_ref[s, 2 * EDGE : SPAN, at], low], axis=0).astype(BF16)

    gps = [
        jnp.concatenate([own(s, slice(WIDTH, CHANNELS)), ddt_ref[s]], axis=1) for s in range(2)
    ]
    for i in range(PAIRS):
        at = slice(i * 128, i * 128 + 128)
        other = slice((PAIRS - 1 - i) * 128, (PAIRS - i) * 128)
        hid_flip = mm(hid_ref[:, other], flip).astype(BF16)
        gw_ref[at] = (mm_tn(hid_ref[:, at], gps[0]) + mm_tn(hid_flip, gps[1])).astype(gw_ref.dtype)
        a = (own(0, at).astype(F32) + mm_nt(gps[0], w_ref[at])).astype(BF16)
        b = (own(1, at).astype(F32) + mm_nt(gps[1], wr_ref[at])).astype(BF16)
        gh_ref[:, at] = (a.astype(F32) + b.astype(F32)).astype(BF16)
        gc_ref[:, at] = gf_ref[0, :, at] + exact(gf_ref[1, :, other], mirror(F32))
    gc_ref[:, WIDTH:] = gf_ref[0, :, WIDTH:] + gf_ref[1, :, WIDTH:]


def call(body, outs, scratch=()):
    return pl.pallas_call(
        body,
        out_shape=[jax.ShapeDtypeStruct(s, t) for s, t in outs],
        scratch_shapes=[pltpu.VMEM(s, F32) for s in scratch],
        compiler_params=pltpu.CompilerParams(vmem_limit_bytes=48 * 1024 * 1024),
    )


SQ4 = (4, 128, 128)
SQ2 = (2, 128, 128)


def per_device(hidden, grad_out, w_proj, conv_w, a_log, dt_bias):
    hid, go = hidden[0], grad_out[0]
    assert hidden.shape[:2] == (1, SPAN)
    size = lax.axis_size("seq")
    up = [(i, i + 1) for i in range(size - 1)]
    down = [(i + 1, i) for i in range(size - 1)]
    before = lax.ppermute(hid[SPAN - EDGE :], "seq", up)
    after = lax.ppermute(hid[:EDGE], "seq", down)
    x_ext = jnp.concatenate([before, hid, after], axis=0)
    w_pad = jnp.pad(w_proj, ((0, 0), (0, 256 - w_proj.shape[1])))
    w_full = lax.all_gather(w_pad, "zero", axis=0, tiled=True)
    conv_full = lax.all_gather(conv_w, "zero", axis=1, tiled=True)
    filters = jnp.pad(conv_full.astype(F32), ((0, 8 - KERNEL), (0, 0)))
    alog = jnp.pad(a_log, (0, 128 - HEADS))[None]
    bias = jnp.pad(dt_bias, (0, 128 - HEADS))[None]
    pieces = (4, PAIRS, STATE, 128)
    state, gstate, dec, w_rev, bcx, dtx, within = call(
        first_kernel,
        [
            (pieces, F32), (pieces, F32), ((4, 16, 128), F32), ((WIDTH, 256), BF16),
            ((2, EXT, 128), F32), (SQ2, F32), (SQ4, F32),
        ],
        [SQ4, SQ4, SQ4],
    )(x_ext, go, w_full, filters, alog, bias)
    dec = dec[:, :PAIRS, None, :]
    own_up = jnp.stack([state[0], state[2], gstate[1], gstate[3]])
    own_down = jnp.stack([state[1], state[3], gstate[0], gstate[2]])
    dec_up = jnp.stack([dec[0], dec[2], dec[1], dec[3]])
    dec_down = jnp.stack([dec[1], dec[3], dec[0], dec[2]])
    in_up = in_down = None
    for hop in range(size - 1):
        out_up, out_down = own_up, own_down
        if hop:
            out_up = own_up + dec_up * in_up.astype(F32)
            out_down = own_down + dec_down * in_down.astype(F32)
        in_up = lax.ppermute(out_up.astype(BF16), "seq", up)
        in_down = lax.ppermute(out_down.astype(BF16), "seq", down)
    s_in = jnp.stack([in_up[0], in_down[0], in_up[1], in_down[1]])
    g_in = jnp.stack([in_down[2], in_up[2], in_down[3], in_up[3]])
    output, gi, gf, ddt, heads = call(
        main_kernel,
        [
            ((SPAN, WIDTH), BF16), ((2, EXT, CHANNELS), F32), ((2, 8, CHANNELS), F32),
            (SQ2, BF16), ((8, 128), F32),
        ],
        [
            SQ4, SQ4, SQ4, SQ4, SQ2, SQ4, SQ4, (4, 128, STATE), (4, 128, STATE), SQ4, SQ4,
            SQ2, SQ2, (4, 2, 128, STATE),
        ],
    )(x_ext, go, filters, alog, bcx, dtx, within, s_in, g_in)
    rim_before = lax.ppermute(gi[:, EDGE + SPAN :].astype(BF16), "seq", up)
    rim_after = lax.ppermute(gi[:, :EDGE].astype(BF16), "seq", down)
    grad_hidden, gw, gc = call(
        last_kernel,
        [((SPAN, WIDTH), BF16), ((WIDTH, 256), F32), ((8, CHANNELS), F32)],
    )(hid, w_full, w_rev, gi, rim_before, rim_after, ddt, gf)
    gw = gw[:, : w_proj.shape[1]].astype(BF16)
    part_w = lax.psum_scatter(gw, "zero", scatter_dimension=0, tiled=True)
    part_c = lax.psum_scatter(gc[:KERNEL].astype(BF16), "zero", scatter_dimension=1, tiled=True)
    share_w, share_c = lax.psum((part_w, part_c), "seq")
    grad_heads = lax.psum(heads[:2, :HEADS], ("seq", "zero"))
    return (output[None], grad_hidden[None], share_w.astype(F32), share_c.astype(F32), grad_heads)


def solution(mesh):
    return jax.shard_map(
        per_device,
        mesh=mesh,
        in_specs=(
            P(("grp", "zero"), "seq", None),
            P(("grp", "zero"), "seq", None),
            P("zero", None),
            P(None, "zero"),
            P(),
            P(),
        ),
        out_specs=(
            P(("grp", "zero"), "seq", None),
            P(("grp", "zero"), "seq", None),
            P(("grp", "zero"), None),
            P("grp", "zero"),
            P("grp", None),
        ),
        check_vma=False,
    )
```

time: 808 us -> 218 us (0.27); the launches traced: 793 us -> 218 us
  blocking collectives: 276 us -> 54.3 us
  local copies, waits for them, and re-layouts: 219 us -> 6.88 us
  other arithmetic: 139 us -> 2.26 us
  matrix products: 75.8 us -> 0 us
  waiting for transfers between devices: 36.3 us -> 82.4 us
  Pallas kernels: 0 us -> 29.6 us
    all_gather x14 -> x2, blocking collectives: 233 us -> 13 us  [the longest x1 7.89 us: per_device(): w_full = lax.all_gather(w_pad, 'zero', axis=0, tiled=True)]
    dot_general x54 -> x0, matrix products: 64.9 us -> none  [the longest x12 20.9 us: conv_core(): jnp.einsum('khij,kjhp->kihp', weights, values, preferred_element_type=jnp...]
    slice x19 -> x9, local copies, waits for them, and re-layouts: 51.2 us -> 2.05 us  [the longest x1 0.92 us: per_device(): gw = gw[:, :w_proj.shape[1]].astype(BF16)]
    ppermute x8 -> x10, waiting for transfers between devices: 0.02 us -> 45.1 us  [the longest x3 36 us: per_device(): in_up = lax.ppermute(out_up.astype(BF16), 'seq', up)]
    add x26 -> x0, other arithmetic: 34 us -> none  [the longest x12 22.9 us: combine_states(): later[0][..., None, None] * earlier[1] + later[1]]
    unnamed x530 -> x15, local copies, waits for them, and re-layouts: 38.1 us -> 4.79 us
    pallas_call x0 -> x3, Pallas kernels: none -> 29.6 us  [the longest x1 22.1 us: per_device(): call(main_kernel, [((SPAN, WIDTH), BF16), ((2, EXT, CHANNELS), F32), ((2,...]
    reduce_sum x17 -> x0, other arithmetic: 28.5 us -> none  [the longest x4 6.75 us: conv_core(): within + offsets[:, :, None]]
  transfers between devices with their start and end apart: 11 -> 13, of which waited for: 2 -> 8; matrix products, arithmetic and copies ran while one was open for 19% -> 2% of each run, Pallas kernels for 0% -> 0%
where the time goes in v1:
time: 218 us
  waiting for transfers between devices  82.4 us (38%)
  blocking collectives  54.3 us (25%)
  Pallas kernels  29.6 us (14%)
  starting transfers between devices  28.4 us (13%)
  between operations  14.1 us (6%)
  local copies, waits for them, and re-layouts  6.88 us (3%)
  other arithmetic  2.26 us (1%)
    ppermute x3, waiting for transfers between devices, per_device(): in_up = lax.ppermute(out_up.astype(BF16), 'seq', up)  36 us
    psum x1, blocking collectives, per_device(): grad_heads = lax.psum(heads[:2, :HEADS], ('seq', 'zero'))  32.9 us
    pallas_call x1, Pallas kernels, per_device(): call(main_kernel, [((SPAN, WIDTH), BF16), ((2, EXT, CHANNELS), F32), ((2,...  22.1 us
    reduce_scatter x1, waiting for transfers between devices, per_device(): part_w = lax.psum_scatter(gw, 'zero', scatter_dimension=0, tiled=True)  19.8 us
    psum x1, waiting for transfers between devices, per_device(): share_w, share_c = lax.psum((part_w, part_c), 'seq')  17.5 us
    ppermute x3, starting transfers between devices, per_device(): in_up = lax.ppermute(out_up.astype(BF16), 'seq', up)  13.4 us
    psum x1, blocking collectives, per_device(): share_w, share_c = lax.psum((part_w, part_c), 'seq')  8.41 us
    all_gather x1, blocking collectives, per_device(): w_full = lax.all_gather(w_pad, 'zero', axis=0, tiled=True)  7.89 us
  transfers between devices with their start and end apart: 13, of which 8 were waited for; matrix products, arithmetic and copies ran while one was open for 2% of the time, Pallas kernels for 0%

profile of v1, /device:TPU:0, one launch (start us, length us, event | category | flops | bytes accessed | tf_op | source)
XLA Modules:
  0.0 217.9 jit_solution(4201975035810792887)
XLA Ops:
  7.3 0.8 slice_bitcast_fusion.1
  8.1 4.9 %collective-permute-start = (bf16[8,1280]{1,0:T(8,128)(2,1)S(1)}, bf16[8,1280]{1,0:T(8,128)(2,1)S(1)}, u32[]{:S(2)}, u32[]{:S(2)}) collective-permute-start(bf16[8,1280]{1,0:T(8,128)(2,1)S(1)} %get-tuple-element.63), channel_id=1, source_target_pairs={{0,4},{4,8},{8,12},{1,5},{5,9},{9,13},{2,6},{6,10},{10,14},{3,7},{... | collective-permute-start | bytes 61448 | tf_op jit(solution)/shard_map/ppermute | solution.py:382
  13.0 1.3 collective-permute-start.1
  14.3 1.0 copy.15
  15.4 7.9 %all_gather.7.w_ref = bf16[1280,256]{1,0:T(8,128)(2,1)S(1)} all-gather(bf16[320,256]{1,0:T(8,128)(2,1)S(1)} %pad.20), channel_id=1, replica_groups=mesh['grp'=2,'seq'=4,'zero'=4] {'zero'}, dimensions={0}, use_global_device_ids=true | all-gather | bytes 819200 | tf_op jit(solution)/shard_map/all_gather | solution.py:386
  23.3 5.1 %all-gather = bf16[4,352,4]{1,2,0:T(4,128)(2,1)S(1)} all-gather(bf16[1,352,4]{1,2,0:T(4,128)(2,1)S(1)} %bitcast.39), channel_id=1, replica_groups=mesh['grp'=2,'seq'=4,'zero'=4] {'zero'}, dimensions={0}, use_global_device_ids=true | all-gather | bytes 14080 | tf_op jit(solution)/shard_map/all_gather | solution.py:387
  28.7 5.1 %shard_map.101 = (f32[4,10,64,128]{3,2,1,0:T(8,128)S(1)}, f32[4,10,64,128]{3,2,1,0:T(8,128)S(1)}, f32[4,16,128]{2,1,0:T(8,128)S(1)}, bf16[1280,256]{1,0:T(8,128)...) custom-call(bf16[144,1280]{1,0:T(8,128)(2,1)S(1)} %pad_maximum_fusion.4.x_ref, ...), custom_call_target="tpu_custom_call" | custom-call | tf_op jit(solution)/shard_map/pallas_call | solution.py:392
  34.1 4.6 %collective-permute-start.2 = (bf16[4,10,64,128]{3,2,1,0:T(8,128)(2,1)S(1)}, bf16[4,10,64,128]{3,2,1,0:T(8,128)(2,1)S(1)}, u32[]{:S(2)}, u32[]{:S(2)}) collective-permute-start(bf16[4,10,64,128]{3,2,1,0:T(8,128)(2,1)S(1)} %fusion.1), channel_id=1, source_target_pairs={{0,4},{4,8},{8,12},{1,5},{5,9},{9,13},{2,6},{6,10},{10,14},{3,7},{... | collective-permute-start | bytes 1966088 | tf_op jit(solution)/shard_map/ppermute | solution.py:411
  38.8 1.3 collective-permute-start.5
  40.1 12.9 %collective-permute-done.2 = bf16[4,10,64,128]{3,2,1,0:T(8,128)(2,1)S(1)} collective-permute-done((bf16[4,10,64,128]{3,2,1,0:T(8,128)(2,1)S(1)}, bf16[4,10,64,128]{3,2,1,0:T(8,128)(2,1)S(1)}, u32[]{:S(2)}, u32[]{:S(2)}) %collective-permute-start.2) | collective-permute-done | bytes 655392 | tf_op jit(solution)/shard_map/ppermute | solution.py:411
  53.3 4.4 %collective-permute-start.3 = (bf16[4,10,64,128]{3,2,1,0:T(8,128)(2,1)S(1)}, bf16[4,10,64,128]{3,2,1,0:T(8,128)(2,1)S(1)}, u32[]{:S(2)}, u32[]{:S(2)}) collective-permute-start(bf16[4,10,64,128]{3,2,1,0:T(8,128)(2,1)S(1)} %add_convert_fusion.3), channel_id=1, source_target_pairs={{0,4},{4,8},{8,12},{1,5},{5,9},{9,13},{2,6},{6,10},{10,14},{3,7},{... | collective-permute-start | bytes 1966088 | tf_op jit(solution)/shard_map/ppermute | solution.py:411
  58.1 1.3 collective-permute-start.6
  59.4 12.0 %collective-permute-done.3 = bf16[4,10,64,128]{3,2,1,0:T(8,128)(2,1)S(1)} collective-permute-done((bf16[4,10,64,128]{3,2,1,0:T(8,128)(2,1)S(1)}, bf16[4,10,64,128]{3,2,1,0:T(8,128)(2,1)S(1)}, u32[]{:S(2)}, u32[]{:S(2)}) %collective-permute-start.3) | collective-permute-done | bytes 655392 | tf_op jit(solution)/shard_map/ppermute | solution.py:411
  71.7 4.4 %collective-permute-start.4 = (bf16[4,10,64,128]{3,2,1,0:T(8,128)(2,1)S(1)}, bf16[4,10,64,128]{3,2,1,0:T(8,128)(2,1)S(1)}, u32[]{:S(2)}, u32[]{:S(2)}) collective-permute-start(bf16[4,10,64,128]{3,2,1,0:T(8,128)(2,1)S(1)} %add_convert_fusion.2), channel_id=1, source_target_pairs={{0,4},{4,8},{8,12},{1,5},{5,9},{9,13},{2,6},{6,10},{10,14},{3,7},{... | collective-permute-start | bytes 1966088 | tf_op jit(solution)/shard_map/ppermute | solution.py:411
  76.4 1.3 collective-permute-start.7
  77.7 11.1 %collective-permute-done.4 = bf16[4,10,64,128]{3,2,1,0:T(8,128)(2,1)S(1)} collective-permute-done((bf16[4,10,64,128]{3,2,1,0:T(8,128)(2,1)S(1)}, bf16[4,10,64,128]{3,2,1,0:T(8,128)(2,1)S(1)}, u32[]{:S(2)}, u32[]{:S(2)}) %collective-permute-start.4) | collective-permute-done | bytes 655392 | tf_op jit(solution)/shard_map/ppermute | solution.py:411
  88.8 4.4 %collective-permute-done.7 = bf16[4,10,64,128]{3,2,1,0:T(8,128)(2,1)S(1)} collective-permute-done((bf16[4,10,64,128]{3,2,1,0:T(8,128)(2,1)S(1)}, bf16[4,10,64,128]{3,2,1,0:T(8,128)(2,1)S(1)}, u32[]{:S(2)}, u32[]{:S(2)}) %collective-permute-start.7) | collective-permute-done | bytes 655392 | tf_op jit(solution)/shard_map/ppermute | solution.py:412
  93.4 22.1 %shard_map.102 = (bf16[128,1280]{1,0:T(8,128)(2,1)}, f32[2,144,1408]{2,1,0:T(8,128)S(1)}, f32[2,8,1408]{2,1,0:T(8,128)S(1)}, bf16[2,128,128]{2,1,0:T(8,128)(2,1)S(1)}, f32[8,128]{1,0:T(8,128)S(1)}) custom-call(bf16[144,1280]{1,0:T(8,128)(2,1)S(1)} %pad_maximum_fusion.4.x_ref, bf16[128,1280]{1,0:T(8,128)(2,1)S(1)} %bitcast.35, ...), custom_call_target="tpu_custom_call" | custom-call | tf_op jit(solution)/shard_map/pallas_call | solution.py:415
  115.6 3.5 %collective-permute-start.8 = (bf16[2,8,1408]{2,1,0:T(8,128)(2,1)S(1)}, bf16[2,8,1408]{2,1,0:T(8,128)(2,1)S(1)}, u32[]{:S(2)}, u32[]{:S(2)}) collective-permute-start(bf16[2,8,1408]{2,1,0:T(8,128)(2,1)S(1)} %get-tuple-element.54), channel_id=1, source_target_pairs={{0,4},{4,8},{8,12},{1,5},{5,9},{9,13},{2,6},{6,10},{10,14},{3,7},{... | collective-permute-start | bytes 135176 | tf_op jit(solution)/shard_map/ppermute | solution.py:426
  119.1 1.3 collective-permute-start.9
  120.4 0.4 collective-permute-done.8.before_ref
  120.8 4.2 %collective-permute-done.9.after_ref = bf16[2,8,1408]{2,1,0:T(8,128)(2,1)S(1)} collective-permute-done((bf16[2,8,1408]{2,1,0:T(8,128)(2,1)S(1)}, bf16[2,8,1408]{2,1,0:T(8,128)(2,1)S(1)}, u32[]{:S(2)}, u32[]{:S(2)}) %collective-permute-start.9) | collective-permute-done | bytes 45088 | tf_op jit(solution)/shard_map/ppermute | solution.py:427
  125.0 2.4 %shard_map.103 = (bf16[128,1280]{1,0:T(8,128)(2,1)}, f32[1280,256]{1,0:T(8,128)S(1)}, f32[8,1408]{1,0:T(8,128)S(1)}) custom-call(bf16[128,1280]{1,0:T(8,128)(2,1)S(1)} %bitcast.33, bf16[1280,256]{1,0:T(8,128)(2,1)S(1)} %all_gather.7.w_ref, bf16[1280,256]{1,0:T(8,128)(2,1)S(1)} %get-tuple-element.27.wr_ref, f32[2,144,1408]{2,1,0:T(8,128)S(1)} %get-tuple-element.28.gi_ref, ...), custom_call_target="tpu_custom_call" | custom-call | tf_op jit(solution)/shard_map/pallas_call | solution.py:428
  127.5 0.9 slice.165
  128.5 1.0 copy.17
  129.5 19.8 %reduce-scatter.5.cloned.1.call-done = bf16[320,148]{1,0:T(8,128)(2,1)} async-done(((bf16[1280,148]{1,0:T(8,128)(2,1)}), bf16[320,148]{1,0:T(8,128)(2,1)}) %reduce-scatter.5.cloned.1.call-update) | async-done | bytes 94736 | tf_op jit(solution)/shard_map/reduce_scatter | solution.py:433
  149.3 32.9 %psum.23 = f32[2,20]{1,0:T(2,128)} all-reduce(f32[2,20]{1,0:T(2,128)S(1)} %slice.144), channel_id=1, replica_groups=mesh['grp'=2,'seq'=4,'zero'=4] {'seq','zero'}, use_global_device_ids=true, to_apply=%region_4.5 | all-reduce | flops 40 | bytes 320 | tf_op jit(solution)/shard_map/psum | solution.py:436
  182.2 1.0 copy.18
  183.2 8.4 %psum.22 = bf16[4,352]{1,0:T(4,128)(2,1)S(1)} all-reduce(bf16[4,352]{1,0:T(4,128)(2,1)S(1)} %copy.18), channel_id=1, replica_groups=mesh['grp'=2,'seq'=4,'zero'=4] {'seq'}, use_global_device_ids=true, to_apply=%region_3.4 | all-reduce | flops 1408 | bytes 5632 | tf_op jit(solution)/shard_map/psum | solution.py:435
  191.6 0.6 convert_element_type.59
  192.2 17.5 %all-reduce.6.cloned.1.call-done = bf16[320,148]{1,0:T(8,128)(2,1)} async-done(((bf16[320,148]{1,0:T(8,128)(2,1)}), bf16[320,148]{1,0:T(8,128)(2,1)}) %all-reduce.6.cloned.1.call-update) | async-done | bytes 94736 | tf_op jit(solution)/shard_map/psum | solution.py:435
  209.7 1.7 copy.16
  (45 shorter events, 2.3 us)
Async XLA Ops:
  7.2 21.4 %copy-start = (bf16[1,128,1280]{2,1,0:T(8,128)(2,1)S(1)}, bf16[1,128,1280]{2,1,0:T(8,128)(2,1)}, u32[]{:S(2)}) copy-start(bf16[1,128,1280]{2,1,0:T(8,128)(2,1)} %param.6) | copy-start | bytes 983044
  7.2 16.1 %copy-start.2 = (bf16[4,352]{1,0:T(4,128)(2,1)S(1)}, bf16[4,352]{1,0:T(4,128)(2,1)}, u32[]{:S(2)}) copy-start(bf16[4,352]{1,0:T(4,128)(2,1)} %param.9) | copy-start | bytes 8452
  7.2 21.4 %copy-start.3 = (f32[20]{0:T(128)S(1)}, f32[20]{0:T(128)}, u32[]{:S(2)}) copy-start(f32[20]{0:T(128)} %param.10) | copy-start | bytes 244
  7.2 21.4 %copy-start.4 = (f32[20]{0:T(128)S(1)}, f32[20]{0:T(128)}, u32[]{:S(2)}) copy-start(f32[20]{0:T(128)} %param.11) | copy-start | bytes 244
  7.2 21.4 %copy-start.1 = (bf16[1,128,1280]{2,1,0:T(8,128)(2,1)S(1)}, bf16[1,128,1280]{2,1,0:T(8,128)(2,1)}, u32[]{:S(2)}) copy-start(bf16[1,128,1280]{2,1,0:T(8,128)(2,1)} %param.7) | copy-start | bytes 983044
  7.2 142.1 %reduce-scatter.5.cloned.1.call-start = ((), (), s32[]{:S(2)}) async-start(), calls=%async_computation.2 | async-start | bytes 819200 | tf_op jit(solution)/shard_map/reduce_scatter | solution.py:433
  8.1 20.5 %collective-permute-start = (bf16[8,1280]{1,0:T(8,128)(2,1)S(1)}, bf16[8,1280]{1,0:T(8,128)(2,1)S(1)}, u32[]{:S(2)}, u32[]{:S(2)}) collective-permute-start(bf16[8,1280]{1,0:T(8,128)(2,1)S(1)} %get-tuple-element.63), channel_id=1, source_target_pairs={{0,4},{4,8},{8,12},{1,5},{5,9},{9,13},{2,6},{6,10},{10,14},{3,7},{... | collective-permute-start | bytes 61448 | tf_op jit(solution)/shard_map/ppermute | solution.py:382
  13.0 15.6 %collective-permute-start.1 = (bf16[8,1280]{1,0:T(8,128)(2,1)S(1)}, bf16[8,1280]{1,0:T(8,128)(2,1)S(1)}, u32[]{:S(2)}, u32[]{:S(2)}) collective-permute-start(bf16[8,1280]{1,0:T(8,128)(2,1)S(1)} %get-tuple-element.64), channel_id=1, source_target_pairs={{4,0},{8,4},{12,8},{5,1},{9,5},{13,9},{6,2},{10,6},{14,10},{7,3},{... | collective-permute-start | bytes 61448 | tf_op jit(solution)/shard_map/ppermute | solution.py:383
  34.1 19.0 %collective-permute-start.2 = (bf16[4,10,64,128]{3,2,1,0:T(8,128)(2,1)S(1)}, bf16[4,10,64,128]{3,2,1,0:T(8,128)(2,1)S(1)}, u32[]{:S(2)}, u32[]{:S(2)}) collective-permute-start(bf16[4,10,64,128]{3,2,1,0:T(8,128)(2,1)S(1)} %fusion.1), channel_id=1, source_target_pairs={{0,4},{4,8},{8,12},{1,5},{5,9},{9,13},{2,6},{6,10},{10,14},{3,7},{... | collective-permute-start | bytes 1966088 | tf_op jit(solution)/shard_map/ppermute | solution.py:411
  38.8 19.0 %collective-permute-start.5 = (bf16[4,10,64,128]{3,2,1,0:T(8,128)(2,1)S(1)}, bf16[4,10,64,128]{3,2,1,0:T(8,128)(2,1)S(1)}, u32[]{:S(2)}, u32[]{:S(2)}) collective-permute-start(bf16[4,10,64,128]{3,2,1,0:T(8,128)(2,1)S(1)} %fusion), channel_id=1, source_target_pairs={{4,0},{8,4},{12,8},{5,1},{9,5},{13,9},{6,2},{10,6},{14,10},{7,3},{... | collective-permute-start | bytes 1966088 | tf_op jit(solution)/shard_map/ppermute | solution.py:412
  53.3 18.0 %collective-permute-start.3 = (bf16[4,10,64,128]{3,2,1,0:T(8,128)(2,1)S(1)}, bf16[4,10,64,128]{3,2,1,0:T(8,128)(2,1)S(1)}, u32[]{:S(2)}, u32[]{:S(2)}) collective-permute-start(bf16[4,10,64,128]{3,2,1,0:T(8,128)(2,1)S(1)} %add_convert_fusion.3), channel_id=1, source_target_pairs={{0,4},{4,8},{8,12},{1,5},{5,9},{9,13},{2,6},{6,10},{10,14},{3,7},{... | collective-permute-start | bytes 1966088 | tf_op jit(solution)/shard_map/ppermute | solution.py:411
  58.1 18.0 %collective-permute-start.6 = (bf16[4,10,64,128]{3,2,1,0:T(8,128)(2,1)S(1)}, bf16[4,10,64,128]{3,2,1,0:T(8,128)(2,1)S(1)}, u32[]{:S(2)}, u32[]{:S(2)}) collective-permute-start(bf16[4,10,64,128]{3,2,1,0:T(8,128)(2,1)S(1)} %add_convert_fusion.1), channel_id=1, source_target_pairs={{4,0},{8,4},{12,8},{5,1},{9,5},{13,9},{6,2},{10,6},{14,10},{7,3},{... | collective-permute-start | bytes 1966088 | tf_op jit(solution)/shard_map/ppermute | solution.py:412
  71.7 17.1 %collective-permute-start.4 = (bf16[4,10,64,128]{3,2,1,0:T(8,128)(2,1)S(1)}, bf16[4,10,64,128]{3,2,1,0:T(8,128)(2,1)S(1)}, u32[]{:S(2)}, u32[]{:S(2)}) collective-permute-start(bf16[4,10,64,128]{3,2,1,0:T(8,128)(2,1)S(1)} %add_convert_fusion.2), channel_id=1, source_target_pairs={{0,4},{4,8},{8,12},{1,5},{5,9},{9,13},{2,6},{6,10},{10,14},{3,7},{... | collective-permute-start | bytes 1966088 | tf_op jit(solution)/shard_map/ppermute | solution.py:411
  76.4 16.8 %collective-permute-start.7 = (bf16[4,10,64,128]{3,2,1,0:T(8,128)(2,1)S(1)}, bf16[4,10,64,128]{3,2,1,0:T(8,128)(2,1)S(1)}, u32[]{:S(2)}, u32[]{:S(2)}) collective-permute-start(bf16[4,10,64,128]{3,2,1,0:T(8,128)(2,1)S(1)} %add_convert_fusion), channel_id=1, source_target_pairs={{4,0},{8,4},{12,8},{5,1},{9,5},{13,9},{6,2},{10,6},{14,10},{7,3},{... | collective-permute-start | bytes 1966088 | tf_op jit(solution)/shard_map/ppermute | solution.py:412
  115.6 5.2 %collective-permute-start.8 = (bf16[2,8,1408]{2,1,0:T(8,128)(2,1)S(1)}, bf16[2,8,1408]{2,1,0:T(8,128)(2,1)S(1)}, u32[]{:S(2)}, u32[]{:S(2)}) collective-permute-start(bf16[2,8,1408]{2,1,0:T(8,128)(2,1)S(1)} %get-tuple-element.54), channel_id=1, source_target_pairs={{0,4},{4,8},{8,12},{1,5},{5,9},{9,13},{2,6},{6,10},{10,14},{3,7},{... | collective-permute-start | bytes 135176 | tf_op jit(solution)/shard_map/ppermute | solution.py:426
  119.1 5.9 %collective-permute-start.9 = (bf16[2,8,1408]{2,1,0:T(8,128)(2,1)S(1)}, bf16[2,8,1408]{2,1,0:T(8,128)(2,1)S(1)}, u32[]{:S(2)}, u32[]{:S(2)}) collective-permute-start(bf16[2,8,1408]{2,1,0:T(8,128)(2,1)S(1)} %get-tuple-element.53), channel_id=1, source_target_pairs={{4,0},{8,4},{12,8},{5,1},{9,5},{13,9},{6,2},{10,6},{14,10},{7,3},{... | collective-permute-start | bytes 135176 | tf_op jit(solution)/shard_map/ppermute | solution.py:427
  128.4 53.8 %reduce-scatter.7.cloned.1.call-start = ((), (), s32[]{:S(2)}) async-start(), calls=%async_computation.4 | async-start | bytes 450560
  129.5 80.2 %all-reduce.6.cloned.1.call-start = ((), (), s32[]{:S(2)}) async-start(), calls=%async_computation.3 | async-start | bytes 327680 | tf_op jit(solution)/shard_map/psum | solution.py:435
Sparse Core Ops, SparseCore 0:
  128.5 20.7 reduce-scatter.4
  151.8 20.6 reduce-scatter.6
  174.9 34.7 all-reduce.5

commit v2 on v1

--- a/solution.py
+++ b/solution.py
@@ -102,7 +102,7 @@
 
 def first_kernel(
     x_ref, go_ref, w_ref, f_ref, alog_ref, bias_ref,
-    state_ref, gstate_ref, dec_ref, wr_ref, bcx_ref, dtx_ref, within_ref,
+    up_ref, down_ref, dup_ref, ddown_ref, wr_ref, bcx_ref, dtx_ref, within_ref,
     tow_t, e_col, bc_t,
 ):
     flip = mirror()
@@ -130,7 +130,9 @@
             bc_t[c] = act.T
             tow_t[c] = (jnp.exp(last_row(within, d) - within) * delta).T
             e_col[c] = jnp.exp(within)
-            dec_ref[c] = jnp.zeros((16, 128), F32)
+
+    own_refs = (up_ref, down_ref)
+    dec_refs = (dup_ref, ddown_ref)
 
     def pair_step(i, carry):
         x = x_ref[:, lanes(i)].astype(F32)
@@ -152,19 +154,23 @@
                 [b_t * tow_t[c, pl.ds(h, 1), :] for h in heads], axis=0
             ).astype(BF16)
             st = mm(bw, values)
-            state_ref[c, i] = jnp.where(low_half, st[:STATE], st[STATE:])
+            own_refs[d][i, s] = jnp.where(low_half, st[:STATE], st[STATE:])
             e = e_col[c]
             e0, e1 = [col(e, h) for h in heads]
             e_pair = jnp.where(low, e0, e1)
-            gstate_ref[c, i] = mm(bc_t[c, STATE:128].astype(BF16), (e_pair * g).astype(BF16))
-            dec_ref[c, pl.ds(i, 1), :] = last_row(e_pair, d)
+            own_refs[1 - d][i, 2 + s] = mm(
+                bc_t[c, STATE:128].astype(BF16), (e_pair * g).astype(BF16)
+            )
+            decay = jnp.broadcast_to(last_row(e_pair, d), (8, 128))
+            dec_refs[d][i, s] = decay
+            dec_refs[1 - d][i, 2 + s] = decay
         return carry
 
     lax.fori_loop(0, PAIRS, pair_step, 0)
 
 
 def main_kernel(
-    x_ref, go_ref, f_ref, alog_ref, bcx_ref, dtx_ref, within_ref, sin_ref, gin_ref,
+    x_ref, go_ref, f_ref, alog_ref, bcx_ref, dtx_ref, within_ref, up_ref, down_ref,
     out_ref, gi_ref, gf_ref, ddt_ref, heads_ref,
     e_col, f_col, tow, within_t, delta_t, score, d_score, d_b, d_c, d_l, d_lt, d_dc, d_dt, bc_act,
 ):
@@ -239,7 +245,8 @@
                     es.append(col(e_all, h))
                 e_pair = jnp.where(low, es[0], es[1])
                 ge = (e_pair * g).astype(BF16)
-                s_in, g_in = sin_ref[c, i], gin_ref[c, i]
+                ahead, behind = (up_ref, down_ref) if d == 0 else (down_ref, up_ref)
+                s_in, g_in = ahead[i, s], behind[i, 2 + s]
                 y_two = mm(jnp.concatenate(ws, axis=0), values)
                 inter = mm(c_mat.astype(BF16), s_in) * e_pair
                 y = y + jnp.where(low, y_two[:128], y_two[128:]) + inter
@@ -334,15 +341,233 @@
     heads_ref[...] = jnp.concatenate([d_alog, d_bias, jnp.zeros((6, 128), F32)], axis=0)
 
 
+MESH = pl.DeviceIdType.MESH
+
+
+def greet_all(sizes):
+    barrier = pltpu.get_barrier_semaphore()
+    for axis, size in sizes:
+        me = lax.axis_index(axis)
+        for k in range(1, size):
+            pl.semaphore_signal(
+                barrier, inc=1, device_id={axis: lax.rem(me + k, size)}, device_id_type=MESH
+            )
+    pl.semaphore_wait(barrier, sum(size - 1 for _, size in sizes))
+
+
+def push(src, dst, send, recv, axis, peer):
+    return pltpu.make_async_remote_copy(
+        src_ref=src,
+        dst_ref=dst,
+        send_sem=send,
+        recv_sem=recv,
+        device_id={axis: peer},
+        device_id_type=MESH,
+    )
+
+
+def greet_sides(me, count, more=0):
+    barrier = pltpu.get_barrier_semaphore()
+    for k in (1, count - 1):
+        pl.semaphore_signal(
+            barrier, inc=1, device_id={"seq": lax.rem(me + k, count)}, device_id_type=MESH
+        )
+    pl.semaphore_wait(barrier, 2 + more)
+
+
+def gather_kernel(
+    shards, count, hid_ref, w_ref, c_ref, x_ref, w_out, f_out,
+    w_slots, c_own, c_slots, before, after, send, recv, sides,
+):
+    seq, zero = lax.axis_index("seq"), lax.axis_index("zero")
+    barrier = pltpu.get_barrier_semaphore()
+    for k in range(1, shards):
+        pl.semaphore_signal(
+            barrier, inc=1, device_id={"zero": lax.rem(zero + k, shards)}, device_id_type=MESH
+        )
+    greet_sides(seq, count, shards - 1)
+    up = push(
+        hid_ref.at[pl.ds(SPAN - 2 * EDGE, 2 * EDGE)], before, sides.at[0], sides.at[1], "seq",
+        lax.rem(seq + 1, count),
+    )
+    down = push(
+        hid_ref.at[pl.ds(0, 2 * EDGE)], after, sides.at[2], sides.at[3], "seq",
+        lax.rem(seq + count - 1, count),
+    )
+
+    @pl.when(seq < count - 1)
+    def _():
+        up.start()
+
+    @pl.when(seq > 0)
+    def _():
+        down.start()
+
+    c_own[...] = jnp.zeros_like(c_own)
+    c_own[:KERNEL] = c_ref[...].astype(F32)
+    copies = []
+    for k in range(1, shards):
+        peer = lax.rem(zero + k, shards)
+        copies.append(push(w_ref, w_slots.at[zero], send.at[k, 0], recv.at[k, 0], "zero", peer))
+        copies.append(push(c_own, c_slots.at[zero], send.at[k, 1], recv.at[k, 1], "zero", peer))
+    for copy in copies:
+        copy.start()
+    w_slots[zero] = w_ref[...]
+    c_slots[zero] = c_own[...]
+    w_out[:, 128:] = jnp.zeros((WIDTH, 128), BF16)
+    x_ref[EDGE : EDGE + SPAN] = hid_ref[...]
+
+    @pl.when(seq == 0)
+    def _():
+        x_ref[:EDGE] = jnp.zeros((EDGE, WIDTH), BF16)
+
+    @pl.when(seq > 0)
+    def _():
+        up.wait_recv()
+        x_ref[:EDGE] = before[EDGE:]
+
+    @pl.when(seq == count - 1)
+    def _():
+        x_ref[EDGE + SPAN :] = jnp.zeros((EDGE, WIDTH), BF16)
+
+    @pl.when(seq < count - 1)
+    def _():
+        down.wait_recv()
+        x_ref[EDGE + SPAN :] = after[:EDGE]
+
+    for copy in copies:
+        copy.wait()
+    rows, columns = w_ref.shape
+    part = c_ref.shape[1]
+    for z in range(shards):
+        w_out[z * rows : (z + 1) * rows, :columns] = w_slots[z]
+        f_out[:, z * part : (z + 1) * part] = c_slots[z]
+
+    @pl.when(seq < count - 1)
+    def _():
+        up.wait_send()
+
+    @pl.when(seq > 0)
+    def _():
+        down.wait_send()
+
+
+def chain_kernel(
+    count, own_up, own_down, dec_up, dec_down, in_up, in_down,
+    out_up, out_down, send, recv,
+):
+    me = lax.axis_index("seq")
+    greet_sides(me, count)
+
+    @pl.when(me == 0)
+    def _():
+        in_up[...] = jnp.zeros_like(in_up)
+
+    @pl.when(me == count - 1)
+    def _():
+        in_down[...] = jnp.zeros_like(in_down)
+
+    ways = (
+        (own_up, dec_up, in_up, out_up, me > 0, me < count - 1, lax.rem(me + 1, count)),
+        (
+            own_down, dec_down, in_down, out_down, me < count - 1, me > 0,
+            lax.rem(me + count - 1, count),
+        ),
+    )
+    sends = []
+    for chunk in range(PAIRS // 2):
+        at = pl.ds(2 * chunk, 2)
+        for way, (own, dec, into, out, hears, tells, peer) in enumerate(ways):
+            copy = push(
+                out.at[at], into.at[at], send.at[way, chunk], recv.at[way, chunk], "seq", peer
+            )
+            sends.append((copy, tells))
+
+            @pl.when(hears)
+            def _():
+                copy.wait_recv()
+
+            @pl.when(tells)
+            def _():
+                for i in (2 * chunk, 2 * chunk + 1):
+                    for q in range(4):
+                        carried = dec[i, q, 0:1] * into[i, q].astype(F32)
+                        out[i, q] = (own[i, q] + carried).astype(BF16)
+                copy.start()
+
+    for copy, tells in sends:
+
+        @pl.when(tells)
+        def _():
+            copy.wait_send()
+
+
 def last_kernel(
-    hid_ref, w_ref, wr_ref, gi_ref, before_ref, after_ref, ddt_ref, gf_ref,
-    gh_ref, gw_ref, gc_ref,
+    shards, count, fold,
+    hid_ref, w_ref, wr_ref, gi_ref, ddt_ref, gf_ref, heads_ref,
+    gh_ref, gw_ref, gc_ref, gd_ref,
+    before, after, parts, part_in, mine, chunk_in, full, total, small, small_in, small2, small2_in,
+    taps, sides, zs, zr, ss, sr,
 ):
+    seq, zero = lax.axis_index("seq"), lax.axis_index("zero")
+    rows = WIDTH // shards
+    fold_rows = rows // fold
+    chunk = mine.shape[0] // count
+    greet_all((("zero", shards), ("seq", count)))
+    up = push(
+        gi_ref.at[:, pl.ds(EDGE + SPAN, EDGE)], before, sides.at[0], sides.at[1], "seq",
+        lax.rem(seq + 1, count),
+    )
+    down = push(
+        gi_ref.at[:, pl.ds(0, EDGE)], after, sides.at[2], sides.at[3], "seq",
+        lax.rem(seq + count - 1, count),
+    )
+
+    @pl.when(seq < count - 1)
+    def _():
+        up.start()
+
+    @pl.when(seq > 0)
+    def _():
+        down.start()
+
+    @pl.when(seq == 0)
+    def _():
+        before[...] = jnp.zeros_like(before)
+
+    @pl.when(seq == count - 1)
+    def _():
+        after[...] = jnp.zeros_like(after)
+
     flip = mirror()
+    small[...] = jnp.zeros_like(small)
+    for i in range(PAIRS):
+        at = slice(i * 128, i * 128 + 128)
+        other = slice((PAIRS - 1 - i) * 128, (PAIRS - i) * 128)
+        block = gf_ref[0, :, at] + exact(gf_ref[1, :, other], mirror(F32))
+        small[KERNEL * i : KERNEL * i + KERNEL] = block[:KERNEL]
+    block = gf_ref[0, :, WIDTH:] + gf_ref[1, :, WIDTH:]
+    small[KERNEL * PAIRS : KERNEL * PAIRS + KERNEL] = block[:KERNEL]
+    small[KERNEL * PAIRS + KERNEL : KERNEL * PAIRS + KERNEL + 2] = heads_ref[:2]
+    first = []
+    for k in range(1, shards):
+        peer = lax.rem(zero + k, shards)
+        copy = push(small, small_in.at[zero], zs.at[1, k], zr.at[1, k], "zero", peer)
+        copy.start()
+        first.append(copy)
+    small_in[zero] = small[...]
+
+    @pl.when(seq > 0)
+    def _():
+        up.wait_recv()
+
+    @pl.when(seq < count - 1)
+    def _():
+        down.wait_recv()
 
     def own(s, at):
-        top = gi_ref[s, EDGE : 2 * EDGE, at] + before_ref[s, :, at].astype(F32)
-        low = gi_ref[s, SPAN : SPAN + EDGE, at] + after_ref[s, :, at].astype(F32)
+        top = gi_ref[s, EDGE : 2 * EDGE, at] + before[s, :, at]
+        low = gi_ref[s, SPAN : SPAN + EDGE, at] + after[s, :, at]
         return jnp.concatenate([top, gi_ref[s, 2 * EDGE : SPAN, at], low], axis=0).astype(BF16)
 
     gps = [
@@ -352,20 +577,110 @@
         at = slice(i * 128, i * 128 + 128)
         other = slice((PAIRS - 1 - i) * 128, (PAIRS - i) * 128)
         hid_flip = mm(hid_ref[:, other], flip).astype(BF16)
-        gw_ref[at] = (mm_tn(hid_ref[:, at], gps[0]) + mm_tn(hid_flip, gps[1])).astype(gw_ref.dtype)
+        total[at] = mm_tn(hid_ref[:, at], gps[0]) + mm_tn(hid_flip, gps[1])
+    for z in range(shards):
+        parts[z, :rows] = total[z * rows : (z + 1) * rows, :128].astype(BF16)
+        folded = jnp.zeros((fold_rows, 128), F32)
+        for q in range(fold):
+            start = z * rows + q * fold_rows
+            piece = total[start : start + fold_rows, 128:]
+            folded = folded + (pltpu.roll(piece, 32 * q, 1) if q else piece)
+        parts[z, rows : rows + fold_rows] = folded.astype(BF16)
+        spare = parts.shape[1] - rows - fold_rows
+        if spare:
+            parts[z, rows + fold_rows :] = jnp.zeros((spare, 128), BF16)
+    scatter = []
+    for k in range(1, shards):
+        peer = lax.rem(zero + k, shards)
+        copy = push(parts.at[peer], part_in.at[k], zs.at[0, k], zr.at[0, k], "zero", peer)
+        copy.start()
+        scatter.append(copy)
+    for copy in first:
+        copy.wait()
+    small2[...] = small_in[0]
+    for z in range(1, shards):
+        small2[...] += small_in[z]
+    second = []
+    for k in range(1, count):
+        peer = lax.rem(seq + k, count)
+        copy = push(small2, small2_in.at[seq], ss.at[0, k], sr.at[0, k], "seq", peer)
+        copy.start()
+        second.append(copy)
+    small2_in[seq] = small2[...]
+    for i in range(PAIRS):
+        at = slice(i * 128, i * 128 + 128)
         a = (own(0, at).astype(F32) + mm_nt(gps[0], w_ref[at])).astype(BF16)
         b = (own(1, at).astype(F32) + mm_nt(gps[1], wr_ref[at])).astype(BF16)
         gh_ref[:, at] = (a.astype(F32) + b.astype(F32)).astype(BF16)
-        gc_ref[:, at] = gf_ref[0, :, at] + exact(gf_ref[1, :, other], mirror(F32))
-    gc_ref[:, WIDTH:] = gf_ref[0, :, WIDTH:] + gf_ref[1, :, WIDTH:]
-
-
-def call(body, outs, scratch=()):
+    for copy in scatter:
+        copy.wait()
+    summed = parts[zero].astype(F32)
+    for k in range(1, shards):
+        summed = summed + part_in[k].astype(F32)
+    mine[...] = summed.astype(BF16)
+    third = []
+    for k in range(1, count):
+        peer = lax.rem(seq + k, count)
+        src = mine.at[pl.ds(pl.multiple_of(peer * chunk, 16), chunk)]
+        copy = push(src, chunk_in.at[k], ss.at[1, k], sr.at[1, k], "seq", peer)
+        copy.start()
+        third.append(copy)
+    for copy in third:
+        copy.wait()
+    here = pl.ds(pl.multiple_of(seq * chunk, 16), chunk)
+    summed = mine[here].astype(F32)
+    for k in range(1, count):
+        summed = summed + chunk_in[k].astype(F32)
+    full[here] = summed.astype(BF16)
+    third = []
+    for k in range(1, count):
+        peer = lax.rem(seq + k, count)
+        copy = push(full.at[here], full.at[here], ss.at[2, k], sr.at[2, k], "seq", peer)
+        copy.start()
+        third.append(copy)
+    for copy in second:
+        copy.wait()
+    summed = small2_in[0]
+    for z in range(1, count):
+        summed = summed + small2_in[z]
+    gd_ref[...] = summed[KERNEL * PAIRS + KERNEL : KERNEL * PAIRS + KERNEL + 2, :HEADS]
+    for i in range(PAIRS + 1):
+        taps[:, i * 128 : i * 128 + 128] = summed[KERNEL * i : KERNEL * i + KERNEL]
+    width = gc_ref.shape[1]
+    for z in range(shards):
+
+        @pl.when(zero == z)
+        def _():
+            gc_ref[...] = taps[:, z * width : (z + 1) * width]
+
+    for copy in third:
+        copy.wait()
+
+    @pl.when(seq < count - 1)
+    def _():
+        up.wait_send()
+
+    @pl.when(seq > 0)
+    def _():
+        down.wait_send()
+
+    gw_ref[:, :128] = full[:rows].astype(F32)
+    tail = full[rows : rows + fold_rows].astype(F32)
+    for q in range(fold):
+        gw_ref[q * fold_rows : (q + 1) * fold_rows, 128:] = tail[:, 32 * q : 32 * q + HEADS]
+
+
+def call(body, outs, scratch=(), sems=(), number=None):
     return pl.pallas_call(
         body,
         out_shape=[jax.ShapeDtypeStruct(s, t) for s, t in outs],
-        scratch_shapes=[pltpu.VMEM(s, F32) for s in scratch],
-        compiler_params=pltpu.CompilerParams(vmem_limit_bytes=48 * 1024 * 1024),
+        scratch_shapes=[pltpu.VMEM(s, t) for s, t in scratch]
+        + [pltpu.SemaphoreType.DMA(s) for s in sems],
+        compiler_params=pltpu.CompilerParams(
+            vmem_limit_bytes=48 * 1024 * 1024,
+            collective_id=number,
+            has_side_effects=number is not None,
+        ),
     )
 
 
@@ -376,42 +691,37 @@
 def per_device(hidden, grad_out, w_proj, conv_w, a_log, dt_bias):
     hid, go = hidden[0], grad_out[0]
     assert hidden.shape[:2] == (1, SPAN)
-    size = lax.axis_size("seq")
-    up = [(i, i + 1) for i in range(size - 1)]
-    down = [(i + 1, i) for i in range(size - 1)]
-    before = lax.ppermute(hid[SPAN - EDGE :], "seq", up)
-    after = lax.ppermute(hid[:EDGE], "seq", down)
-    x_ext = jnp.concatenate([before, hid, after], axis=0)
-    w_pad = jnp.pad(w_proj, ((0, 0), (0, 256 - w_proj.shape[1])))
-    w_full = lax.all_gather(w_pad, "zero", axis=0, tiled=True)
-    conv_full = lax.all_gather(conv_w, "zero", axis=1, tiled=True)
-    filters = jnp.pad(conv_full.astype(F32), ((0, 8 - KERNEL), (0, 0)))
+    count, shards = lax.axis_size("seq"), lax.axis_size("zero")
+    rows = WIDTH // shards
+    part = CHANNELS // shards
     alog = jnp.pad(a_log, (0, 128 - HEADS))[None]
     bias = jnp.pad(dt_bias, (0, 128 - HEADS))[None]
-    pieces = (4, PAIRS, STATE, 128)
-    state, gstate, dec, w_rev, bcx, dtx, within = call(
+    x_ext, w_full, filters = call(
+        functools.partial(gather_kernel, shards, count),
+        [((EXT, WIDTH), BF16), ((WIDTH, 256), BF16), ((8, CHANNELS), F32)],
+        [
+            ((shards,) + w_proj.shape, BF16), ((8, part), F32), ((shards, 8, part), F32),
+            ((2 * EDGE, WIDTH), BF16), ((2 * EDGE, WIDTH), BF16),
+        ],
+        [(shards, 2), (shards, 2), (4,)],
+        0,
+    )(hid, w_proj, conv_w)
+    pieces = (PAIRS, 4, STATE, 128)
+    own_up, own_down, dec_up, dec_down, w_rev, bcx, dtx, within = call(
         first_kernel,
         [
-            (pieces, F32), (pieces, F32), ((4, 16, 128), F32), ((WIDTH, 256), BF16),
-            ((2, EXT, 128), F32), (SQ2, F32), (SQ4, F32),
+            (pieces, F32), (pieces, F32), ((PAIRS, 4, 8, 128), F32), ((PAIRS, 4, 8, 128), F32),
+            ((WIDTH, 256), BF16), ((2, EXT, 128), F32), (SQ2, F32), (SQ4, F32),
         ],
-        [SQ4, SQ4, SQ4],
+        [(SQ4, F32)] * 3,
     )(x_ext, go, w_full, filters, alog, bias)
-    dec = dec[:, :PAIRS, None, :]
-    own_up = jnp.stack([state[0], state[2], gstate[1], gstate[3]])
-    own_down = jnp.stack([state[1], state[3], gstate[0], gstate[2]])
-    dec_up = jnp.stack([dec[0], dec[2], dec[1], dec[3]])
-    dec_down = jnp.stack([dec[1], dec[3], dec[0], dec[2]])
-    in_up = in_down = None
-    for hop in range(size - 1):
-        out_up, out_down = own_up, own_down
-        if hop:
-            out_up = own_up + dec_up * in_up.astype(F32)
-            out_down = own_down + dec_down * in_down.astype(F32)
-        in_up = lax.ppermute(out_up.astype(BF16), "seq", up)
-        in_down = lax.ppermute(out_down.astype(BF16), "seq", down)
-    s_in = jnp.stack([in_up[0], in_down[0], in_up[1], in_down[1]])
-    g_in = jnp.stack([in_down[2], in_up[2], in_down[3], in_up[3]])
+    in_up, in_down = call(
+        functools.partial(chain_kernel, count),
+        [(pieces, BF16), (pieces, BF16)],
+        [(pieces, BF16), (pieces, BF16)],
+        [(2, PAIRS // 2), (2, PAIRS // 2)],
+        1,
+    )(own_up, own_down, dec_up, dec_down)
     output, gi, gf, ddt, heads = call(
         main_kernel,
         [
@@ -419,22 +729,34 @@
             (SQ2, BF16), ((8, 128), F32),
         ],
         [
-            SQ4, SQ4, SQ4, SQ4, SQ2, SQ4, SQ4, (4, 128, STATE), (4, 128, STATE), SQ4, SQ4,
-            SQ2, SQ2, (4, 2, 128, STATE),
+            (s, F32)
+            for s in (
+                SQ4, SQ4, SQ4, SQ4, SQ2, SQ4, SQ4, (4, 128, STATE), (4, 128, STATE), SQ4, SQ4,
+                SQ2, SQ2, (4, 2, 128, STATE),
+            )
         ],
-    )(x_ext, go, filters, alog, bcx, dtx, within, s_in, g_in)
-    rim_before = lax.ppermute(gi[:, EDGE + SPAN :].astype(BF16), "seq", up)
-    rim_after = lax.ppermute(gi[:, :EDGE].astype(BF16), "seq", down)
-    grad_hidden, gw, gc = call(
-        last_kernel,
-        [((SPAN, WIDTH), BF16), ((WIDTH, 256), F32), ((8, CHANNELS), F32)],
-    )(hid, w_full, w_rev, gi, rim_before, rim_after, ddt, gf)
-    gw = gw[:, : w_proj.shape[1]].astype(BF16)
-    part_w = lax.psum_scatter(gw, "zero", scatter_dimension=0, tiled=True)
-    part_c = lax.psum_scatter(gc[:KERNEL].astype(BF16), "zero", scatter_dimension=1, tiled=True)
-    share_w, share_c = lax.psum((part_w, part_c), "seq")
-    grad_heads = lax.psum(heads[:2, :HEADS], ("seq", "zero"))
-    return (output[None], grad_hidden[None], share_w.astype(F32), share_c.astype(F32), grad_heads)
+    )(x_ext, go, filters, alog, bcx, dtx, within, in_up, in_down)
+    fold = 4 if rows % 64 == 0 else 1
+    step = 16 * count
+    padded = -(-(rows + rows // fold) // step) * step
+    lines = 48
+    grad_hidden, share_w, share_c, grad_heads = call(
+        functools.partial(last_kernel, shards, count, fold),
+        [
+            ((SPAN, WIDTH), BF16), (w_proj.shape, F32), ((KERNEL, part), F32), ((2, HEADS), F32),
+        ],
+        [
+            ((2, EDGE, CHANNELS), F32), ((2, EDGE, CHANNELS), F32),
+            ((shards, padded, 128), BF16), ((shards, padded, 128), BF16),
+            ((padded, 128), BF16), ((count, padded // count, 128), BF16), ((padded, 128), BF16),
+            ((WIDTH, 256), F32),
+            ((lines, 128), F32), ((shards, lines, 128), F32),
+            ((lines, 128), F32), ((count, lines, 128), F32), ((KERNEL, CHANNELS), F32),
+        ],
+        [(4,), (2, shards), (2, shards), (3, count), (3, count)],
+        2,
+    )(hid, w_full, w_rev, gi, ddt, gf, heads)
+    return (output[None], grad_hidden[None], share_w, share_c, grad_heads)
 
 
 def solution(mesh):

time: 218 us -> 195 us (0.89)
  Pallas kernels: 29.6 us -> 187 us
  waiting for transfers between devices: 82.4 us -> 0 us
  blocking collectives: 54.3 us -> 0 us
  starting transfers between devices: 28.4 us -> 0 us
  between operations: 14.1 us -> 0.71 us
  other arithmetic: 2.26 us -> 0 us
    pallas_call x2 -> x4, Pallas kernels: 7.5 us -> 165 us  [the longest x1 126 us: per_device(): call(functools.partial(chain_kernel, count), [(pieces, BF16), (pieces, BF...]
    ppermute x10 -> x0, waiting for transfers between devices: 45.1 us -> none  [the longest x3 36 us: per_device(): in_up = lax.ppermute(out_up.astype(BF16), 'seq', up)]
    psum x2 -> x0, blocking collectives: 41.3 us -> none  [the longest x1 32.9 us: per_device(): grad_heads = lax.psum(heads[:2, :HEADS], ('seq', 'zero'))]
    ppermute x10 -> x0, starting transfers between devices: 28.3 us -> none  [the longest x3 13.4 us: per_device(): in_up = lax.ppermute(out_up.astype(BF16), 'seq', up)]
    reduce_scatter x1 -> x0, waiting for transfers between devices: 19.8 us -> none  [per_device(): part_w = lax.psum_scatter(gw, 'zero', scatter_dimension=0, tiled=True)]
    psum x1 -> x0, waiting for transfers between devices: 17.5 us -> none  [per_device(): share_w, share_c = lax.psum((part_w, part_c), 'seq')]
    all_gather x2 -> x0, blocking collectives: 13 us -> none  [the longest x1 7.89 us: per_device(): w_full = lax.all_gather(w_pad, 'zero', axis=0, tiled=True)]
    unnamed x15 -> x13, local copies, waits for them, and re-layouts: 4.79 us -> 6.35 us
  transfers between devices with their start and end apart: 13 -> 0, of which waited for: 8 -> 0; matrix products, arithmetic and copies ran while one was open for 2% -> 0% of each run, Pallas kernels for 0% -> 0%
where the time goes in v2:
time: 195 us
  Pallas kernels  187 us (96%)
  local copies, waits for them, and re-layouts  7.02 us (4%)
    pallas_call x1, Pallas kernels, per_device(): call(functools.partial(chain_kernel, count), [(pieces, BF16), (pieces, BF...  126 us
    pallas_call x1, Pallas kernels, per_device(): call(main_kernel, [((SPAN, WIDTH), BF16), ((2, EXT, CHANNELS), F32), ((2,...  22.1 us
    pallas_call x1, Pallas kernels, per_device(): call(functools.partial(last_kernel, shards, count, fold), [((SPAN, WIDTH)...  21 us
    pallas_call x1, Pallas kernels, per_device(): call(functools.partial(gather_kernel, shards, count), [((EXT, WIDTH), BF1...  12.9 us
    unnamed x13, local copies, waits for them, and re-layouts  6.35 us
    pallas_call x1, Pallas kernels, per_device(): call(first_kernel, [(pieces, F32), (pieces, F32), ((PAIRS, 4, 8, 128), F3...  5.06 us

profile of v2, /device:TPU:0, one launch (start us, length us, event | category | flops | bytes accessed | tf_op | source)
XLA Modules:
  0.0 194.9 jit_solution(17165676162176616030)
XLA Ops:
  0.6 0.7 pad_bitcast_fusion
  1.3 1.0 copy.11.w_ref
  2.3 0.0 copy-start.2
  2.3 1.0 copy-done.2
  3.3 0.0 copy-start.3
  3.3 0.7 copy-done.3
  4.0 12.9 %shard_map.101 = (bf16[144,1280]{1,0:T(8,128)(2,1)S(1)}, bf16[1280,256]{1,0:T(8,128)(2,1)S(1)}, f32[8,1408]{1,0:T(8,128)S(1)}) custom-call(bf16[128,1280]{1,0:T(8,128)(2,1)S(1)} %bitcast.10, bf16[320,148]{1,0:T(8,128)(2,1)S(1)} %copy.11.w_ref, bf16[4,352]{1,0:T(4,128)(2,1)S(1)} %copy-done.3), custom_call_target="tpu_custom_call" | custom-call | tf_op jit(solution)/shard_map/pallas_call | solution.py:699
  16.8 0.0 copy-start
  16.9 1.0 copy-done
  17.8 5.1 %shard_map.102 = (f32[10,4,64,128]{3,2,1,0:T(8,128)S(1)}, f32[10,4,64,128]{3,2,1,0:T(8,128)S(1)}, f32[10,4,8,128]{3,2,1,0:T(8,128)S(1)}, f32[10,4,8,128]{3,2,1,0...) custom-call(bf16[144,1280]{1,0:T(8,128)(2,1)S(1)} %get-tuple-element, ...), custom_call_target="tpu_custom_call" | custom-call | tf_op jit(solution)/shard_map/pallas_call | solution.py:710
  22.9 0.0 copy-start.1
  22.9 126.2 %shard_map.103 = (bf16[10,4,64,128]{3,2,1,0:T(8,128)(2,1)S(1)}, bf16[10,4,64,128]{3,2,1,0:T(8,128)(2,1)S(1)}) custom-call(f32[10,4,64,128]{3,2,1,0:T(8,128)S(1)} %get-tuple-element.33.own_up, f32[10,4,64,128]{3,2,1,0:T(8,128)S(1)} %get-tuple-element.34.own_down, f32[10,4,8,128]{3,2,1,0:T(8,128)S(1)} %get-tuple-element.35.dec_up, ...), custom_call_target="tpu_custom_call" | custom-call | tf_op jit(solution)/shard_map/pallas_call | solution.py:718
  149.1 0.0 copy-done.1
  149.1 22.1 %shard_map.104 = (bf16[128,1280]{1,0:T(8,128)(2,1)}, f32[2,144,1408]{2,1,0:T(8,128)S(1)}, f32[2,8,1408]{2,1,0:T(8,128)S(1)}, bf16[2,128,128]{2,1,0:T(8,128)(2,1)S(1)}, f32[8,128]{1,0:T(8,128)S(1)}) custom-call(bf16[144,1280]{1,0:T(8,128)(2,1)S(1)} %get-tuple-element.27.x_ref, bf16[128,1280]{1,0:T(8,128)(2,1)S(1)} %bitcast.9, ...), custom_call_target="tpu_custom_call" | custom-call | tf_op jit(solution)/shard_map/pallas_call | solution.py:725
  171.2 21.0 %shard_map.105 = (bf16[128,1280]{1,0:T(8,128)(2,1)S(1)}, f32[320,148]{1,0:T(8,128)S(1)}, f32[4,352]{1,0:T(4,128)S(1)}, f32[2,20]{1,0:T(2,128)S(1)}) custom-call(bf16[128,1280]{1,0:T(8,128)(2,1)S(1)} %bitcast.11, bf16[1280,256]{1,0:T(8,128)(2,1)S(1)} %get-tuple-element.29.w_ref, bf16[1280,256]{1,0:T(8,128)(2,1)S(1)} %get-tuple-element.40.wr_ref, ...), custom_call_target="tpu_custom_call" | custom-call | tf_op jit(solution)/shard_map/pallas_call | solution.py:743
  192.2 0.8 copy.12
  193.0 0.7 copy.16
  193.7 0.6 copy.17
  194.3 0.6 copy.18
Async XLA Ops:
  2.3 1.0 copy-start.2
  3.3 0.7 copy-start.3
  16.8 1.0 copy-start
  22.9 126.2 %copy-start.1 = (bf16[1,128,1280]{2,1,0:T(8,128)(2,1)S(1)}, bf16[1,128,1280]{2,1,0:T(8,128)(2,1)}, u32[]{:S(2)}) copy-start(bf16[1,128,1280]{2,1,0:T(8,128)(2,1)} %param.7) | copy-start | bytes 983044
